TPU v7x, 32 devices: a whole 2x2x4 slice. The times are simulated.
32 devices in a mesh: wide: 16 (over z, y, core), narrow: 2 (over x).
Axes of the slice: x: 2, y: 2, z: 4, core: 2. Of those that a mesh axis runs over, the one named last changes fastest.
Arguments:
- tokens: bfloat16 [1024, 64, 768], P(('wide', 'narrow')), may hold values from -6 to 6
- cotangent: bfloat16 [1024, 64, 768], P(('wide', 'narrow')), may hold values from -0.3125 to 0.3125
- groups: int32 [512], replicated, may hold values from 0 to 108, as said below
- qkv_weight: bfloat16 [768, 2304], replicated, may hold values from -0.21875 to 0.21875
- query_bias: float32 [768], replicated, may hold values from -1.25 to 1.25
- value_bias: float32 [768], replicated, may hold values from -1.25 to 1.25
- out_weight: bfloat16 [768, 768], replicated, may hold values from -0.625 to 0.625
- out_bias: float32 [768], replicated, may hold values from -1.25 to 1.25
- gain_one: float32 [768], replicated, may hold values from 0.5 to 1.5
- shift_one: float32 [768], replicated, may hold values from -1.25 to 1.25
- up_weight: bfloat16 [768, 3072], replicated, may hold values from -0.21875 to 0.21875
- up_bias: float32 [3072], replicated, may hold values from -1.25 to 1.25
- down_weight: bfloat16 [3072, 768], replicated, may hold values from -0.109375 to 0.109375
- down_bias: float32 [768], replicated, may hold values from -1.25 to 1.25
- gain_two: float32 [768], replicated, may hold values from 0.5 to 1.5
- shift_two: float32 [768], replicated, may hold values from -1.25 to 1.25
Outputs:
- loss: float32 [], replicated
- block_out: bfloat16 [1024, 64, 768], P(('wide', 'narrow'))
- input_grad: float32 [1024, 64, 768], P(('wide', 'narrow'))
- qkv_weight_grad: float32 [768, 2304], P('wide')
- query_bias_grad: float32 [768], P('wide')
- value_bias_grad: float32 [768], P('wide')
- out_weight_grad: float32 [768, 768], P('wide')
- out_bias_grad: float32 [768], P('wide')
- gain_one_grad: float32 [768], P('wide')
- shift_one_grad: float32 [768], P('wide')
- up_weight_grad: float32 [768, 3072], P('wide')
- up_bias_grad: float32 [3072], P('wide')
- down_weight_grad: float32 [3072, 768], P('wide')
- down_bias_grad: float32 [768], P('wide')
- gain_two_grad: float32 [768], P('wide')
- shift_two_grad: float32 [768], P('wide')
Inputs may be any that keep to these rules, and one draw needn't show every extreme that they name: A pair's in-batch negatives are the other pairs of its language group, among 109 groups of uneven size; the pairs of a group may lie anywhere in the batch.
All inputs are finite; a program needn't handle non-finite values.
Results may differ from a plain program's by a relative error of at most 0.014.
Values may be sent and summed in bfloat16 or wider, within the bound.
A program may use at most 320 MiB of HBM per device.

v0:
```python
import functools

import jax
import jax.numpy as jnp
from jax import lax
from jax.experimental import pallas as pl
from jax.experimental.pallas import tpu as pltpu
from jax.sharding import PartitionSpec as P

BF = jnp.bfloat16
F32 = jnp.float32
MESH = pl.DeviceIdType.MESH

HEADS = 12
QUAD = 4
SCALE = 40.0
MARGIN = 0.3
EPS = 1e-06
SIDE = 8
VMEM_BYTES = 60 * 2**20


def nn(a, b):
    return lax.dot_general(a, b, (((1,), (0,)), ((), ())), preferred_element_type=F32)


def nt(a, b):
    return lax.dot_general(a, b, (((1,), (1,)), ((), ())), preferred_element_type=F32)


def tn(a, b):
    return lax.dot_general(a, b, (((0,), (0,)), ((), ())), preferred_element_type=F32)


def params(**more):
    return pltpu.CompilerParams(vmem_limit_bytes=VMEM_BYTES, **more)


def resident(shape):
    return pl.BlockSpec(shape, lambda *_: (0,) * len(shape), pipeline_mode=pl.Buffered(1))


def shape_of(shape, dtype):
    return jax.ShapeDtypeStruct(shape, dtype)


def head_mask(quad):
    head = quad // QUAD
    at = lambda axis: lax.broadcasted_iota(jnp.int32, (quad, quad), axis) // head
    return (at(0) == at(1)).astype(F32).astype(BF)


def line(ref):
    return ref[...].reshape(1, ref.shape[0])


def blocked(rows, mask):
    return jnp.concatenate([rows] * QUAD, axis=0) * mask


def diagonal(full, seq):
    half = full.shape[1] // 2
    lane = lax.broadcasted_iota(jnp.int32, (seq, half), 1) < half // 2
    left = jnp.where(lane, full[:seq, :half], full[seq : 2 * seq, :half])
    right = jnp.where(lane, full[2 * seq : 3 * seq, half:], full[3 * seq :, half:])
    return jnp.concatenate([left, right], axis=1)


def paired(left, right, seq):
    half = left.shape[1] // 2
    lane = lax.broadcasted_iota(jnp.int32, (seq, half), 1) < half // 2
    parts = []
    for at in (slice(0, half), slice(half, 2 * half)):
        full = tn(left[:, at], right[:, at])
        parts.append(jnp.where(lane, full[:seq], full[seq:]))
    return jnp.concatenate(parts, axis=1)


def attend_kernel(x_ref, w_ref, qb_ref, vb_ref, qkv_ref, p_ref, ctx_ref):
    sents, seq, width = x_ref.shape
    rows = x_ref[...].reshape(sents * seq, width)
    quad = width // QUADS
    for part, bias in ((0, qb_ref), (1, None), (2, vb_ref)):
        cols = slice(part * width, (part + 1) * width)
        y = nn(rows, w_ref[:, cols])
        if bias is not None:
            y = y + line(bias)
        qkv_ref[:, cols] = y.astype(BF)
    mask = head_mask(quad)
    scale = (width // HEADS) ** -0.5
    for s in range(sents):
        at = slice(s * seq, (s + 1) * seq)
        for g in range(width // quad):
            q = qkv_ref[at, g * quad : (g + 1) * quad]
            k = qkv_ref[at, width + g * quad : width + (g + 1) * quad]
            v = qkv_ref[at, 2 * width + g * quad : 2 * width + (g + 1) * quad]
            scores = nt(k, blocked(q, mask)) * scale
            e = jnp.exp(scores - jnp.max(scores, axis=0, keepdims=True))
            p = (e * (1.0 / jnp.sum(e, axis=0, keepdims=True))).astype(BF)
            p_ref[s, :, g * quad : (g + 1) * quad] = p
            ctx_ref[at, g * quad : (g + 1) * quad] = diagonal(tn(p, v), seq).astype(BF)


def attend(tokens, qkv_weight, query_bias, value_bias):
    sents, seq, width = tokens.shape
    rows = sents * seq
    side = SIDE * seq
    return pl.pallas_call(
        attend_kernel,
        grid=(sents // SIDE,),
        in_specs=[
            pl.BlockSpec((SIDE, seq, width), lambda i: (i, 0, 0)),
            resident((width, 3 * width)),
            resident((width,)),
            resident((width,)),
        ],
        out_specs=[
            pl.BlockSpec((side, 3 * width), lambda i: (i, 0)),
            pl.BlockSpec((SIDE, seq, width), lambda i: (i, 0, 0)),
            pl.BlockSpec((side, width), lambda i: (i, 0)),
        ],
        out_shape=[
            shape_of((rows, 3 * width), BF),
            shape_of((sents, seq, width), BF),
            shape_of((rows, width), BF),
        ],
        compiler_params=params(),
        name="attend",
    )(tokens, qkv_weight, query_bias, value_bias)


def norm(values):
    mean = jnp.mean(values, -1, keepdims=True)
    centred = values - mean
    root = lax.rsqrt(jnp.mean(centred * centred, -1, keepdims=True) + EPS)
    return centred * root, root


def place():
    wide, narrow = lax.axis_index("wide"), lax.axis_index("narrow")
    return wide, narrow, wide // 4, (wide // 2) % 2, wide % 2


def forward_kernel(
    x_ref, ctx_ref, ow_ref, ob_ref, g1_ref, s1_ref, uw_hbm, ub_ref, dw_hbm, db_ref, g2_ref, s2_ref,
    out_ref, low_ref, xh1_ref, rs1_ref, hid_ref, slope_ref, xh2_ref, rs2_ref, cls_ref, all_ref,
    rows_ref, uw_ref, dw_ref, w_sems, buf, zs, zr, ys, yr, xs, xr, cs, cr, done,
):
    sents, part, width = x_ref.shape
    depth = uw_ref.shape[1]
    rows = sents * part
    step = pl.program_id(0)
    wide, narrow, z, y, core = place()
    nz, nx = buf.shape[0], buf.shape[3]
    wide_of = lambda a, b, c: (a * 2 + b) * 2 + c

    z_peers = [(lax.rem(z + k, nz), k) for k in range(1, nz)]
    x_peers = [(lax.rem(narrow + k, nx), k) for k in range(1, nx)]
    z_copies = [
        pltpu.make_async_remote_copy(
            src_ref=buf.at[z, y, core, narrow], dst_ref=buf.at[z, y, core, narrow],
            send_sem=zs.at[k - 1], recv_sem=zr.at[k - 1],
            device_id=(wide_of(to, y, core), narrow), device_id_type=MESH,
        )
        for to, k in z_peers
    ]
    y_copy = pltpu.make_async_remote_copy(
        src_ref=buf.at[:, y, core, narrow], dst_ref=buf.at[:, y, core, narrow],
        send_sem=ys, recv_sem=yr,
        device_id=(wide_of(z, 1 - y, core), narrow), device_id_type=MESH,
    )
    x_copies = [
        pltpu.make_async_remote_copy(
            src_ref=buf.at[:, :, core, narrow], dst_ref=buf.at[:, :, core, narrow],
            send_sem=xs.at[k - 1], recv_sem=xr.at[k - 1],
            device_id=(wide, to), device_id_type=MESH,
        )
        for to, k in x_peers
    ]
    core_copy = pltpu.make_async_remote_copy(
        src_ref=buf.at[:, :, core], dst_ref=buf.at[:, :, core],
        send_sem=cs, recv_sem=cr,
        device_id=(wide_of(z, y, 1 - core), narrow), device_id_type=MESH,
    )

    barrier = pltpu.get_barrier_semaphore()
    weights = [
        pltpu.make_async_copy(uw_hbm, uw_ref, w_sems.at[0]), pltpu.make_async_copy(dw_hbm, dw_ref, w_sems.at[1])
    ]

    @pl.when(step == 0)
    def _():
        for copy in weights:
            copy.start()
        for to, _ in z_peers:
            pl.semaphore_signal(barrier, inc=1, device_id=(wide_of(to, y, core), narrow), device_id_type=MESH)
        pl.semaphore_signal(barrier, inc=1, device_id=(wide_of(z, 1 - y, core), narrow), device_id_type=MESH)
        for to, _ in x_peers:
            pl.semaphore_signal(barrier, inc=1, device_id=(wide, to), device_id_type=MESH)
        pl.semaphore_signal(barrier, inc=1, device_id=(wide_of(z, y, 1 - core), narrow), device_id_type=MESH)
        pl.semaphore_wait(barrier, nz + nx)

    block = lambda ref: ref[...].reshape(rows, ref.shape[2])

    def put(ref, value):
        ref[...] = value.astype(ref.dtype).reshape(ref.shape)

    pre_one = block(x_ref).astype(F32) + nn(block(ctx_ref), ow_ref[...]) + line(ob_ref)
    xh1, rs1 = norm(pre_one)
    normed = xh1 * line(g1_ref) + line(s1_ref)
    low = normed.astype(BF)
    put(low_ref, low)
    put(xh1_ref, xh1)
    put(rs1_ref, jnp.broadcast_to(rs1, (rows, 128)))
    total = normed + line(db_ref)

    @pl.when(step == 0)
    def _():
        for copy in weights:
            copy.wait()

    for c in range(depth // width):
        cols = slice(c * width, (c + 1) * width)
        up = nn(low, uw_ref[:, cols]) + ub_ref[cols].reshape(1, width)
        cdf = 0.5 * (lax.erf(up * 0.7071067811865476) + 1.0)
        slope = cdf + up * (0.3989422804014327 * jnp.exp(-0.5 * up * up))
        hidden = (up * cdf).astype(BF)
        hid_ref[:, :, cols] = hidden.reshape(sents, part, width)
        slope_ref[:, :, cols] = slope.astype(BF).reshape(sents, part, width)
        total = total + nn(hidden, dw_ref[cols, :])
    xh2, rs2 = norm(total)
    final = xh2 * line(g2_ref) + line(s2_ref)
    put(out_ref, final)
    put(xh2_ref, xh2)
    put(rs2_ref, jnp.broadcast_to(rs2, (rows, 128)))

    @pl.when(step == 0)
    def _():
        for s in range(sents):
            cls_ref[s : s + 1, :] = final[s * part : s * part + 1, :]
        cls = cls_ref[...]
        pooled = cls * lax.rsqrt(jnp.sum(cls * cls, -1, keepdims=True) + EPS)
        for s in range(sents):
            half = slice(s % 2 * width, (s % 2 + 1) * width)
            rows_ref[s // 2 : s // 2 + 1, half] = pooled[s : s + 1, :]
        buf[z, y, core, narrow] = rows_ref[...].astype(BF)
        for copy in z_copies:
            copy.start()

    @pl.when(step == 1)
    def _():
        for copy in z_copies:
            copy.wait()
        y_copy.start()

    @pl.when(step == 2)
    def _():
        y_copy.wait()
        for copy in x_copies:
            copy.start()

    @pl.when(step == 3)
    def _():
        for copy in x_copies:
            copy.wait()
        core_copy.start()
        core_copy.wait()
        out = pltpu.make_async_copy(buf, all_ref, done)
        out.start()
        out.wait()


def forward(tokens, ctx, ow, ob, g1, s1, uw, ub, dw, db, g2, s2, sizes):
    sents, seq, width = tokens.shape
    depth = uw.shape[1]
    part = seq // 4
    nz, nx = sizes[0] // 4, sizes[1]
    tile = lambda lanes: pl.BlockSpec((sents, part, lanes), lambda i: (0, i, 0))
    whole = lambda lanes, dtype: shape_of((sents, seq, lanes), dtype)
    slots = (nz, 2, 2, nx, sents // 2, 2 * width)
    dma = pltpu.SemaphoreType.DMA
    return pl.pallas_call(
        forward_kernel,
        grid=(4,),
        in_specs=[
            tile(width), tile(width), resident(ow.shape), resident(ob.shape), resident(g1.shape),
            resident(s1.shape), pl.BlockSpec(memory_space=pl.ANY), resident(ub.shape),
            pl.BlockSpec(memory_space=pl.ANY),
            resident(db.shape), resident(g2.shape), resident(s2.shape),
        ],
        out_specs=[
            tile(width), tile(width), tile(width), tile(128), tile(depth), tile(depth), tile(width),
            tile(128), pl.BlockSpec((sents, width), lambda i: (0, 0)), pl.BlockSpec(memory_space=pl.ANY),
        ],
        out_shape=[
            whole(width, BF), whole(width, BF), whole(width, BF), whole(128, F32), whole(depth, BF),
            whole(depth, BF), whole(width, BF), whole(128, F32), shape_of((sents, width), F32),
            shape_of(slots, BF),
        ],
        scratch_shapes=[
            pltpu.VMEM((sents // 2, 2 * width), F32), pltpu.VMEM(uw.shape, BF), pltpu.VMEM(dw.shape, BF), dma((2,)),
            pltpu.VMEM(slots, BF),
            dma((nz - 1,)), dma((nz - 1,)), dma, dma, dma((nx - 1,)), dma((nx - 1,)), dma, dma, dma,
        ],
        compiler_params=params(collective_id=0, has_side_effects=True),
        name="forward",
    )(tokens, ctx.reshape(sents, seq, width), ow, ob, g1, s1, uw, ub, dw, db, g2, s2)


def ranking_kernel(
    all_ref, group_ref, cls_ref, cot_ref, xh2_ref, rs2_ref, g2_ref,
    loss_ref, down_ref, sums_ref, dcls, gcol_ref,
):
    pairs, width = all_ref.shape[0], all_ref.shape[1] // 2
    own = cls_ref.shape[0] // 2
    step = pl.program_id(0)

    @pl.when(step == 0)
    def _():
        first = (lax.axis_index("wide") * lax.axis_size("narrow") + lax.axis_index("narrow")) * own
        strip = min(256, pairs)
        groups = line(group_ref)
        gcol_ref[...] = jnp.transpose(jnp.broadcast_to(groups, (128, pairs)))
        own_rows = pl.ds(pl.multiple_of(first, own), own)

        def logits_of(left, right, start):
            count = left.shape[0]
            same_at = lax.broadcasted_iota(jnp.int32, (count, pairs), 0) + start
            pair_at = lax.broadcasted_iota(jnp.int32, (count, pairs), 1)
            hit = same_at == pair_at
            return nt(left, right) * SCALE - jnp.where(hit, SCALE * MARGIN, 0.0), hit

        def column_lse(left_at, right_at):
            right = all_ref[:, right_at * width : (right_at + 1) * width]

            def strip_step(at, carry):
                top, total, diag = carry
                start = pl.multiple_of(at * strip, strip)
                left = all_ref[pl.ds(start, strip), left_at * width : (left_at + 1) * width]
                logits, hit = logits_of(left, right, start)
                masked = jnp.where(gcol_ref[pl.ds(start, strip), :1] == groups, logits, -1e30)
                peak = jnp.maximum(top, jnp.max(masked, axis=0, keepdims=True))
                total = total * jnp.exp(top - peak) + jnp.sum(jnp.exp(masked - peak), axis=0, keepdims=True)
                diag = diag + jnp.sum(jnp.where(hit, logits, 0.0), axis=0, keepdims=True)
                return peak, total, diag

            start = (jnp.full((1, pairs), -1e30, F32), jnp.zeros((1, pairs), F32), jnp.zeros((1, pairs), F32))
            top, total, diag = lax.fori_loop(0, pairs // strip, strip_step, start)
            return top + jnp.log(total), diag

        col_lse, diag = column_lse(0, 1)
        row_lse, diag_again = column_lse(1, 0)
        loss_ref[...] = jnp.sum(col_lse - diag + row_lse - diag_again, axis=1, keepdims=True) / pairs

        same = gcol_ref[own_rows, :1] == groups

        def side(my_at, other_at, other_lse):
            other = all_ref[:, other_at * width : (other_at + 1) * width]
            mine = all_ref[own_rows, my_at * width : (my_at + 1) * width]
            logits, hit = logits_of(mine, other, first)
            eye = hit.astype(F32)
            masked = jnp.where(same, logits, -1e30)
            e = jnp.exp(masked - jnp.max(masked, axis=1, keepdims=True))
            d_mine = (e / jnp.sum(e, axis=1, keepdims=True) - eye).astype(BF)
            d_other = (jnp.where(same, jnp.exp(masked - other_lse), 0.0) - eye).astype(BF)
            return (nn(d_mine, other) + nn(d_other, other)) * SCALE

        for at, (other, lse) in enumerate(((1, col_lse), (0, row_lse))):
            terms = side(at, other, lse)
            for p in range(own):
                dcls[2 * p + at : 2 * p + at + 1, :] = terms[p : p + 1, :]
        d = dcls[...]
        c = cls_ref[...]
        root = lax.rsqrt(jnp.sum(c * c, -1, keepdims=True) + EPS)
        dcls[...] = root * d - root * root * root * c * jnp.sum(c * d, -1, keepdims=True)
        sums_ref[...] = jnp.zeros_like(sums_ref)

    side_sents, seq, _ = cot_ref.shape
    rows = side_sents * seq
    start = pl.multiple_of(step * side_sents, side_sents)
    extra = dcls[pl.ds(start, side_sents), :]
    at_zero = lax.broadcasted_iota(jnp.int32, (side_sents, seq, width), 1) == 0
    d_final = cot_ref[...].astype(F32) + jnp.where(at_zero, extra[:, None, :], 0.0)
    d_final = d_final.reshape(rows, width)
    xhat = xh2_ref[...].reshape(rows, width).astype(F32)
    root = rs2_ref[...].reshape(rows, 128)[:, :1]
    e = d_final * line(g2_ref)
    d_pre = (e - jnp.mean(e, -1, keepdims=True) - xhat * jnp.mean(e * xhat, -1, keepdims=True)) * root
    d_down = d_pre.astype(BF)
    down_ref[...] = d_down
    sums_ref[0:1, :] += jnp.sum(d_final * xhat, axis=0, keepdims=True)
    sums_ref[1:2, :] += jnp.sum(d_final, axis=0, keepdims=True)
    sums_ref[2:3, :] += jnp.sum(d_down.astype(F32), axis=0, keepdims=True)


def ranking(gathered, groups, cls, cotangent, xh2, rs2, g2):
    sents, seq, width = cotangent.shape
    pairs = gathered.shape[0]
    tile = lambda lanes: pl.BlockSpec((SIDE, seq, lanes), lambda i: (i, 0, 0))
    return pl.pallas_call(
        ranking_kernel,
        grid=(sents // SIDE,),
        in_specs=[
            resident(gathered.shape), resident(groups.shape), resident(cls.shape), tile(width), tile(width), tile(128),
            resident(g2.shape),
        ],
        out_specs=[
            pl.BlockSpec((1, 1), lambda i: (0, 0)),
            pl.BlockSpec((SIDE * seq, width), lambda i: (i, 0)),
            pl.BlockSpec((8, width), lambda i: (0, 0)),
        ],
        out_shape=[shape_of((1, 1), F32), shape_of((sents * seq, width), BF), shape_of((8, width), F32)],
        scratch_shapes=[pltpu.VMEM((sents, width), F32), pltpu.VMEM((pairs, 128), jnp.int32)],
        compiler_params=params(),
        name="ranking",
    )(gathered, groups, cls, cotangent, xh2, rs2, g2)


def copy_to(src, dst, sends, recvs, at, device):
    return pltpu.make_async_remote_copy(
        src_ref=src, dst_ref=dst, send_sem=sends.at[at], recv_sem=recvs.at[at], device_id=device,
        device_id_type=MESH,
    )


def plus(*terms):
    return sum(t.astype(F32) for t in terms).astype(BF)


class Peers:
    def __init__(self, nz):
        self.nz = nz
        wide, self.x, self.z, self.y, self.core = place()
        self.sibling = (wide + 1 - 2 * self.core, self.x)
        self.over_x = (wide, 1 - self.x)
        self.over_y = (wide + 2 - 4 * self.y, self.x)
        self.zs = [lax.rem(self.z + k, nz) for k in range(1, nz)]
        self.over_z = [(lax.rem(wide + 4 * k, 4 * nz), self.x) for k in range(1, nz)]

    def greet(self, devices):
        barrier = pltpu.get_barrier_semaphore()
        for device in devices:
            pl.semaphore_signal(barrier, inc=1, device_id=device, device_id_type=MESH)
        pl.semaphore_wait(barrier, len(devices))


class Stages:
    SEMS = 9

    def __init__(self, peers, terms, got, sends, recvs):
        self.peers, self.terms, self.got, self.sends, self.recvs = peers, terms, got, sends, recvs
        self.third = got["xa"].shape[2]

    @staticmethod
    def scratch(nz, rows, cols):
        third = rows // 3
        return {
            "xa": (nz, 2, third, cols), "yb": (2, nz, rows - third, cols),
            "ya": (nz, third, cols), "xb": (nz, rows - third, cols),
        }

    def first(self):
        p, t = self.peers, self.third
        return [
            copy_to(self.terms.at[1 - p.x, :, :, :t], self.got["xa"], self.sends, self.recvs, 1, p.over_x),
            copy_to(self.terms.at[:, :, 1 - p.y, t:], self.got["yb"], self.sends, self.recvs, 2, p.over_y),
        ]

    def second(self):
        p, t = self.peers, self.third
        return [
            copy_to(self.terms.at[p.x, :, 1 - p.y, :t], self.got["ya"], self.sends, self.recvs, 3, p.over_y),
            copy_to(self.terms.at[1 - p.x, :, p.y, t:], self.got["xb"], self.sends, self.recvs, 4, p.over_x),
        ]

    def add_first(self):
        p, t = self.peers, self.third
        for copy in self.first():
            copy.wait()
        self.terms[p.x, :, :, :t] = plus(self.terms[p.x, :, :, :t], self.got["xa"][...])
        for h in range(2):
            self.terms[h, :, p.y, t:] = plus(self.terms[h, :, p.y, t:], self.got["yb"][h])

    def add_second(self):
        p, t = self.peers, self.third
        for copy in self.second():
            copy.wait()
        self.terms[p.x, :, p.y, :t] = plus(self.terms[p.x, :, p.y, :t], self.got["ya"][...])
        self.terms[p.x, :, p.y, t:] = plus(self.terms[p.x, :, p.y, t:], self.got["xb"][...])


class Finish:
    def __init__(self, peers, shard, got_z, mine, other, sends, recvs):
        self.peers, self.shard, self.got_z, self.mine, self.other = peers, shard, got_z, mine, other
        self.sends, self.recvs = sends, recvs

    def along_z(self):
        p = self.peers
        return [
            copy_to(self.shard(to), self.got_z.at[k], self.sends, self.recvs, 5 + k, device)
            for k, (to, device) in enumerate(zip(p.zs, p.over_z, strict=True))
        ]

    def along_x(self):
        return copy_to(self.mine, self.other, self.sends, self.recvs, 8, self.peers.over_x)

    def add(self):
        for copy in self.along_z():
            copy.wait()
        got = [self.got_z[k] for k in range(self.peers.nz - 1)]
        self.mine[...] = plus(self.shard(self.peers.z)[...], *got)


def hand_out(value, keep, send):
    halves, nz, ny, rows, cols = keep.shape
    core = lax.axis_index("wide") % 2
    for z in range(nz):
        for y in range(ny):
            first = (z * ny + y) * 2 * rows
            for ref, side in ((keep, core), (send, 1 - core)):
                part = value[pl.ds(pl.multiple_of(first + side * rows, rows), rows), :].astype(BF)
                for h in range(halves):
                    ref[h, z, y] = part[:, h * cols : (h + 1) * cols]


def backward_kernel(fused, nz, *refs):
    (down_ref, hid_ref, slope_ref, dw_hbm, uw_hbm, xh1_ref, rs1_ref, g1_ref, ow_ref, actx_ref) = refs[:10]
    (up_ref, attn_ref, ctx_ref, sums_ref, upsum_ref, owg_ref, dwg_ref) = refs[10:17]
    dw_ref, uw_ref, w_sems, owg, *comm = refs[17:]
    blocks = 4
    width = down_ref.shape[1]
    rows, depth = slope_ref.shape
    step = pl.program_id(0)
    weights = [
        pltpu.make_async_copy(dw_hbm, dw_ref, w_sems.at[0]), pltpu.make_async_copy(uw_hbm, uw_ref, w_sems.at[1])
    ]

    if fused:
        terms, send, got, xa, yb, ya, xb, c_send, c_recv, s_send, s_recv = comm
        peers = Peers(nz)
        stages = Stages(peers, terms, {"xa": xa, "yb": yb, "ya": ya, "xb": xb}, s_send, s_recv)

        def exchange(i):
            return copy_to(send.at[i % 2], got.at[i % 2], c_send, c_recv, i, peers.sibling)

    @pl.when(step == 0)
    def _():
        for copy in weights:
            copy.start()
        sums_ref[...] = jnp.zeros_like(sums_ref)
        upsum_ref[...] = jnp.zeros_like(upsum_ref)
        if fused:
            peers.greet([peers.sibling, peers.over_x, peers.over_y])

    def settle(i):
        exchange(i).wait()
        for h in range(2):
            terms[h, i] = plus(terms[h, i], got[i % 2, h, 0])

    @pl.when(step < blocks)
    def _():
        value = tn(hid_ref[...], down_ref[...])
        if fused:

            @pl.when(step > 0)
            def _():
                settle(step - 1)

            owg[...] = value
            hand_out(owg, terms.at[:, pl.ds(step, 1)], send.at[step % 2])
            exchange(step).start()

        else:
            dwg_ref[...] = value.astype(BF)

    @pl.when(step == blocks)
    def _():
        for copy in weights:
            copy.wait()

    @pl.when(step >= blocks)
    def _():
        d_down = down_ref[pl.ds(pl.multiple_of((step - blocks) * rows, rows), rows), :]
        total = d_down.astype(F32)
        for c in range(depth // width):
            cols = slice(c * width, (c + 1) * width)
            d_up = (nt(d_down, dw_ref[cols, :]) * slope_ref[:, cols].astype(F32)).astype(BF)
            up_ref[:, cols] = d_up
            upsum_ref[:, cols] += jnp.sum(d_up.astype(F32), axis=0, keepdims=True)
            total = total + nt(d_up, uw_ref[:, cols])
        xhat = xh1_ref[...].astype(F32)
        root = rs1_ref[:, :1]
        e = total * g1_ref[...].reshape(1, width)
        d_pre = (e - jnp.mean(e, -1, keepdims=True) - xhat * jnp.mean(e * xhat, -1, keepdims=True)) * root
        d_attn = d_pre.astype(BF)
        attn_ref[...] = d_attn
        ctx_ref[...] = nt(d_attn, ow_ref[...]).astype(BF)
        sums_ref[0:1, :] += jnp.sum(total * xhat, axis=0, keepdims=True)
        sums_ref[1:2, :] += jnp.sum(total, axis=0, keepdims=True)
        sums_ref[2:3, :] += jnp.sum(d_attn.astype(F32), axis=0, keepdims=True)
        part = tn(actx_ref[...], d_attn)

        @pl.when(step == blocks)
        def _():
            owg[...] = part

        @pl.when(step > blocks)
        def _():
            owg[...] += part

    if fused:

        @pl.when(step == blocks)
        def _():
            settle(blocks - 1)
            for copy in stages.first():
                copy.start()

        @pl.when(step == blocks + 2)
        def _():
            stages.add_first()
            for copy in stages.second():
                copy.start()

    @pl.when(step == pl.num_programs(0) - 1)
    def _():
        if fused:
            hand_out(owg, owg_ref.at[0], owg_ref.at[1])
            stages.add_second()
            dwg_ref[...] = terms[peers.x, :, peers.y]
        else:
            owg_ref[...] = owg[...].astype(BF)


def backward(d_down, hidden, slope, dw, uw, xh1, rs1, g1, ow, ctx, sizes):
    fused = sizes == (16, 2)
    nz = sizes[0] // 4
    rows, width = d_down.shape
    depth = uw.shape[1]
    side = rows // 4
    tile = lambda lanes: pl.BlockSpec((side, lanes), lambda i: (jnp.maximum(i - 4, 0), 0))
    once = lambda *shape: pl.BlockSpec(shape, lambda i: (0,) * len(shape))
    shard = depth // sizes[0]
    half = width // 2
    dma = pltpu.SemaphoreType.DMA
    scratch = [
        pltpu.VMEM(dw.shape, BF), pltpu.VMEM(uw.shape, BF), dma((2,)), pltpu.VMEM((width, width), F32)
    ]
    if fused:
        scratch += [
            pltpu.VMEM((2, nz, 2, shard, half), BF), pltpu.VMEM((2, 2, 1, 2, shard, half), BF),
            pltpu.VMEM((2, 2, 1, 2, shard, half), BF),
        ]
        scratch += [pltpu.VMEM(s, BF) for s in Stages.scratch(nz, shard, half).values()]
        scratch += [dma((4,)), dma((4,)), dma((Stages.SEMS,)), dma((Stages.SEMS,))]
        dwg_spec, dwg_shape = once(nz, shard, half), (nz, shard, half)
        owg_shape = (2, 2, nz, 2, width // sizes[0], half)
        extra = dict(collective_id=1, has_side_effects=True)
    else:
        dwg_spec, dwg_shape = pl.BlockSpec((width, width), lambda i: (jnp.minimum(i, 3), 0)), (depth, width)
        owg_shape = (width, width)
        extra = {}
    return pl.pallas_call(
        functools.partial(backward_kernel, fused, nz),
        grid=(8,),
        in_specs=[
            resident((rows, width)), pl.BlockSpec((rows, width), lambda i: (0, jnp.minimum(i, 3))), tile(depth),
            pl.BlockSpec(memory_space=pl.ANY), pl.BlockSpec(memory_space=pl.ANY), tile(width), tile(128),
            resident(g1.shape), resident(ow.shape), tile(width),
        ],
        out_specs=[
            tile(depth), tile(width), tile(width), once(8, width), once(1, depth), once(*owg_shape), dwg_spec
        ],
        out_shape=[
            shape_of((rows, depth), BF), shape_of((rows, width), BF), shape_of((rows, width), BF),
            shape_of((8, width), F32), shape_of((1, depth), F32), shape_of(owg_shape, BF),
            shape_of(dwg_shape, BF),
        ],
        scratch_shapes=scratch,
        compiler_params=params(**extra),
        name="backward",
    )(d_down, hidden, slope, dw, uw, xh1, rs1, g1, ow, ctx)


UPS, QUADS, TILES = 4, 3, 4
FIRST_QUAD = UPS
FIRST_INPUT = UPS + QUADS * TILES
STEPS = FIRST_INPUT + TILES
OUT_PIECE, UP_PIECE, QUAD_PIECE = 0, 1, 1 + UPS
PIECES = UPS + 1 + QUADS
VECTORS = 16


def tail_kernel(fused, nz, *refs):
    (low_ref, up_ref, q_ref, k_ref, v_ref, dctx_ref, p_ref, x_ref, w_hbm, owg_ref, dsum_ref,
     one_ref, two_ref, upsum_ref) = refs[:14]
    out_ref, vec_out = refs[14:16]
    if fused:
        outs = refs[16:20]
        w_ref, w_sem, dqkv, acc, vec, *comm = refs[20:]
    else:
        upg_ref, qkvg_ref = refs[16:18]
        w_ref, w_sem, dqkv, acc, vec = refs[18:]
    rows, quad = q_ref.shape
    sents, seq, _ = p_ref.shape
    width = acc.shape[0]
    step = pl.program_id(0)
    weight = pltpu.make_async_copy(w_hbm, w_ref, w_sem)
    at_quad = jnp.clip(step - FIRST_QUAD, 0, QUADS * TILES - 1)
    g, tile = at_quad // TILES, at_quad % TILES

    if fused:
        (mine, other, dmine, dother, terms, send, got, xa, yb, ya, xb, gz, dz, vlow, vgot, sends, recvs, d_sends, d_recvs,
         v_sends, v_recvs) = comm
        peers = Peers(nz)
        down = Finish(peers, lambda at: dsum_ref.at[at], dz, dmine, dother, d_sends, d_recvs)

        def stages_of(n):
            return Stages(
                peers, terms.at[n], {"xa": xa.at[n], "yb": yb.at[n], "ya": ya.at[n], "xb": xb.at[n]}, sends.at[n],
                recvs.at[n],
            )

        def finish_of(n):
            return Finish(
                peers, lambda at: terms.at[n, peers.x, at, peers.y], gz.at[n], mine.at[n], other.at[n],
                sends.at[n], recvs.at[n],
            )

        def chip(n):
            return copy_to(send.at[n % 2], got.at[n % 2], sends.at[n], recvs.at[n], 0, peers.sibling)

        def add_chip(n):
            chip(n).wait()
            for h in range(2):
                terms[n, h] = plus(terms[n, h], got[n % 2, h])
            for copy in stages_of(n).first():
                copy.start()

        def add_first(n):
            stages_of(n).add_first()
            for copy in stages_of(n).second():
                copy.start()

        def add_second(n):
            stages_of(n).add_second()
            for copy in finish_of(n).along_z():
                copy.start()

        def add_z(n):
            finish_of(n).add()
            finish_of(n).along_x().start()

        def last(n):
            finish_of(n).along_x().wait()

        usual, hurried = (1, 3, 5, 7, 8), (1, 2, 3, 4, STEPS)
        ready = [*range(-1, UPS)] + [FIRST_QUAD + TILES * (q + 1) - 1 for q in range(QUADS)]

        def settle():
            for stage, action in enumerate((add_chip, add_first, add_second, add_z, last)):
                at = [t + (hurried if n == PIECES - 1 else usual)[stage] for n, t in enumerate(ready)]
                due, piece = step == at[0], jnp.int32(0)
                for n in range(1, PIECES):
                    due = due | (step == at[n])
                    piece = jnp.where(step == at[n], n, piece)
                pl.when(due)(functools.partial(action, piece))

        def vector_copy(n, device):
            return copy_to(vlow, vgot.at[n], v_sends, v_recvs, n, device)

        routes = [[peers.sibling], [peers.over_x], [peers.over_y], peers.over_z]

        def vector_copies(hop):
            return [vector_copy(hop + k, device) for k, device in enumerate(routes[hop])]

        @pl.when(step == 0)
        def _():
            peers.greet([peers.sibling, peers.over_x, peers.over_y, *peers.over_z])
            for copy in down.along_z():
                copy.start()
            for h in range(2):
                terms[OUT_PIECE, h] = owg_ref[0, h]
                send[OUT_PIECE, h] = owg_ref[1, h]
            chip(OUT_PIECE).start()

    @pl.when(step == 0)
    def _():
        weight.start()
        vec[...] = jnp.zeros_like(vec)
        vec[2:3, :] = one_ref[2:3, :]
        vec[3:5, :] = one_ref[0:2, :]
        vec[5:6, :] = two_ref[2:3, :]
        vec[6:8, :] = two_ref[0:2, :]
        for c in range(UPS):
            vec[8 + c : 9 + c, :] = upsum_ref[:, c * width : (c + 1) * width]

    @pl.when(step < UPS)
    def _():
        value = tn(low_ref[...], up_ref[...])
        if fused:
            acc[...] = value
        else:
            upg_ref[...] = value.astype(BF)

    @pl.when((step >= FIRST_QUAD) & (step < FIRST_INPUT))
    def _():
        mask = head_mask(quad)
        scale = (quad // QUAD) ** -0.5
        here = lambda size, s=0: pl.ds(pl.multiple_of(tile * rows + s * seq, seq), size)
        for s in range(sents):
            at = slice(s * seq, (s + 1) * seq)
            k = k_ref[at, :]
            p_low = p_ref[s]
            p = p_low.astype(F32)
            dctx = blocked(dctx_ref[at, :], mask)
            d_probs = nt(v_ref[at, :], dctx)
            d_scores = (p * (d_probs - jnp.sum(p * d_probs, axis=0, keepdims=True))).astype(BF)
            dqkv[g, here(seq, s), :quad] = (paired(d_scores, k, seq) * scale).astype(BF)
            dqkv[g, here(seq, s), quad : 2 * quad] = (nn(d_scores, blocked(q_ref[at, :], mask)) * scale).astype(BF)
            dqkv[g, here(seq, s), 2 * quad :] = nn(p_low, dctx).astype(BF)
        grads = dqkv[g, here(rows), :]
        part = tn(x_ref[...], grads)
        q_sum = jnp.sum(grads[:, :quad].astype(F32), axis=0, keepdims=True)
        v_sum = jnp.sum(grads[:, 2 * quad :].astype(F32), axis=0, keepdims=True)
        for q in range(QUADS):

            @pl.when(g == q)
            def _(q=q):
                vec[0:1, q * quad : (q + 1) * quad] += q_sum
                vec[1:2, q * quad : (q + 1) * quad] += v_sum

        @pl.when(tile == 0)
        def _():
            acc[...] = part

        @pl.when(tile > 0)
        def _():
            acc[...] += part

    if fused:
        settle()
        done_quad = (step >= FIRST_QUAD) & (step < FIRST_INPUT) & (tile == TILES - 1)

        @pl.when((step < UPS) | done_quad)
        def _():
            n = jnp.where(step < UPS, UP_PIECE + step, QUAD_PIECE + g)
            hand_out(acc, terms.at[n], send.at[n % 2])
            chip(n).start()

        @pl.when(step == FIRST_INPUT - 1)
        def _():
            vlow[...] = vec[...].astype(BF)
            for copy in vector_copies(0):
                copy.start()

        for hop in range(4):

            @pl.when(step == FIRST_INPUT + hop)
            def _(hop=hop):
                for copy in vector_copies(hop):
                    copy.wait()
                vec[...] = vlow[...].astype(F32) + sum(vgot[hop + k].astype(F32) for k in range(len(routes[hop])))
                if hop < 3:
                    vlow[...] = vec[...].astype(BF)
                    for copy in vector_copies(hop + 1):
                        copy.start()

        @pl.when(step == 4)
        def _():
            down.add()
            down.along_x().start()

        @pl.when(step == 7)
        def _():
            down.along_x().wait()

    else:

        @pl.when((step >= FIRST_QUAD) & (step < FIRST_INPUT) & (tile == TILES - 1))
        def _():
            qkvg_ref[...] = acc[...].astype(BF)

    @pl.when(step == FIRST_INPUT)
    def _():
        weight.wait()

    @pl.when(step >= FIRST_INPUT)
    def _():
        here = pl.ds(pl.multiple_of((step - FIRST_INPUT) * rows, rows), rows)
        grads = jnp.concatenate(
            [dqkv[q, here, part * quad : (part + 1) * quad] for part in range(3) for q in range(QUADS)], axis=1
        )
        out_ref[...] = nt(grads, w_ref[...]).astype(BF)

    @pl.when(step == STEPS - 1)
    def _():
        if fused:
            last(PIECES - 1)
        vec_out[...] = vec[...]
        if fused:
            for ref, value in zip(outs, (mine, other, dmine, dother), strict=True):
                ref[...] = value[...]


def tail(low, d_up, qkv, d_ctx, probs, token_rows, qkv_weight, owg, dsum, one, two, upsum, sizes):
    fused = sizes == (16, 2)
    nz = sizes[0] // 4
    sents, seq, width = probs.shape
    rows = sents * seq
    side = rows // TILES
    quad = width // QUADS
    shard, half = width // sizes[0], width // 2
    at = lambda i: jnp.clip(i - FIRST_QUAD, 0, QUADS * TILES - 1)
    cols = lambda part: pl.BlockSpec((side, quad), lambda i: (at(i) % TILES, part * QUADS + at(i) // TILES))
    once = lambda *shape: pl.BlockSpec(shape, lambda i: (0,) * len(shape))
    finish = lambda lanes: pl.BlockSpec((side, lanes), lambda i: (jnp.maximum(i - FIRST_INPUT, 0), 0))
    dma = pltpu.SemaphoreType.DMA
    scratch = [
        pltpu.VMEM(qkv_weight.shape, BF), dma, pltpu.VMEM((QUADS, rows, width), BF),
        pltpu.VMEM((width, width), F32), pltpu.VMEM((VECTORS, width), F32),
    ]
    out_specs = [finish(width), once(VECTORS, width)]
    out_shape = [shape_of((rows, width), BF), shape_of((VECTORS, width), F32)]
    if fused:
        piece = (2, nz, 2, shard, half)
        scratch += [pltpu.VMEM((PIECES, shard, half), BF)] * 2 + [pltpu.VMEM(dsum.shape[1:], BF)] * 2
        scratch += [pltpu.VMEM((PIECES, *piece), BF), pltpu.VMEM((2, *piece), BF), pltpu.VMEM((2, *piece), BF)]
        scratch += [pltpu.VMEM((PIECES, *s), BF) for s in Stages.scratch(nz, shard, half).values()]
        scratch += [
            pltpu.VMEM((PIECES, nz - 1, shard, half), BF), pltpu.VMEM((nz - 1, *dsum.shape[1:]), BF),
            pltpu.VMEM((VECTORS, width), BF), pltpu.VMEM((2 + nz, VECTORS, width), BF),
        ]
        scratch += [dma((PIECES, Stages.SEMS))] * 2 + [dma((Stages.SEMS,))] * 2 + [dma((2 + nz,))] * 2
        out_specs += [once(PIECES, shard, half)] * 2 + [once(*dsum.shape[1:])] * 2
        out_shape += [shape_of((PIECES, shard, half), BF)] * 2 + [shape_of(dsum.shape[1:], BF)] * 2
        extra = dict(collective_id=2, has_side_effects=True)
    else:
        out_specs += [
            pl.BlockSpec((width, width), lambda i: (0, jnp.minimum(i, UPS - 1))),
            pl.BlockSpec((width, width), lambda i: (0, at(i) // TILES)),
        ]
        out_shape += [shape_of((width, UPS * width), BF), shape_of((width, QUADS * width), BF)]
        extra = {}
    return pl.pallas_call(
        functools.partial(tail_kernel, fused, nz),
        grid=(STEPS,),
        in_specs=[
            resident((rows, width)), pl.BlockSpec((rows, width), lambda i: (0, jnp.minimum(i, UPS - 1))),
            cols(0), cols(1), cols(2), cols(0),
            pl.BlockSpec((SIDE, seq, quad), lambda i: (at(i) % TILES, 0, at(i) // TILES)),
            pl.BlockSpec((side, width), lambda i: (at(i) % TILES, 0)),
            pl.BlockSpec(memory_space=pl.ANY), resident(owg.shape), resident(dsum.shape), resident(one.shape),
            resident(two.shape), resident(upsum.shape),
        ],
        out_specs=out_specs,
        out_shape=out_shape,
        scratch_shapes=scratch,
        compiler_params=params(**extra),
        name="tail",
    )(low, d_up, qkv, qkv, qkv, d_ctx, probs, token_rows, qkv_weight, owg, dsum, one, two, upsum)


def finish_kernel(fused, part_ref, attn_ref, *refs):
    if not fused:
        (input_ref,) = refs
    else:
        (mine_ref, other_ref, dmine_ref, dother_ref, vec_ref, input_ref, qkv_ref, qb_ref, vb_ref, out_ref, ob_ref,
         g1_ref, s1_ref, up_ref, ub_ref, down_ref, db_ref, g2_ref, s2_ref) = refs
    input_ref[...] = part_ref[...].astype(F32) + attn_ref[...].astype(F32)
    if not fused:
        return

    @pl.when(pl.program_id(0) == 0)
    def _():
        wide, narrow, z, _, _ = place()
        width = vec_ref.shape[1]
        shard = qb_ref.shape[0]

        def whole(mine, other):
            mine, other = mine.astype(F32), other.astype(F32)
            return jnp.concatenate([jnp.where(narrow == 0, mine, other), jnp.where(narrow == 0, other, mine)], axis=-1)

        for n in range(UPS):
            up_ref[:, n * width : (n + 1) * width] = whole(mine_ref[UP_PIECE + n], other_ref[UP_PIECE + n])
        out_ref[...] = whole(mine_ref[OUT_PIECE], other_ref[OUT_PIECE])
        quad = width // QUADS
        for q in range(QUADS):
            block = whole(mine_ref[QUAD_PIECE + q], other_ref[QUAD_PIECE + q])
            for part in range(3):
                to = part * width + q * quad
                qkv_ref[:, to : to + quad] = block[:, part * quad : (part + 1) * quad]
        down_ref[...] = whole(dmine_ref[...], dother_ref[...])
        rolled = pltpu.roll(vec_ref[...], lax.rem(width - wide * shard, width), 1)
        for n, ref in enumerate((qb_ref, vb_ref, ob_ref, g1_ref, s1_ref, db_ref, g2_ref, s2_ref)):
            ref[...] = rolled[n, :shard]
        depth = ub_ref.shape[0]
        ups = jnp.concatenate([vec_ref[pl.ds(8 + z, 1), :]] * 8, axis=0)
        ub_ref[...] = pltpu.roll(ups, lax.rem(width - lax.rem(wide, 4) * depth, width), 1)[0, :depth]


def finish(part, d_attn, sums, sizes, depth):
    fused = bool(sums)
    rows, width = part.shape
    side = rows // TILES
    shard = width // sizes[0]
    tile = pl.BlockSpec((side, width), lambda i: (i, 0))
    shapes = [(rows, width)]
    if fused:
        up = depth // sizes[0]
        vector = (shard,)
        shapes += [
            (shard, 3 * width), vector, vector, (shard, width), vector, vector, vector, (shard, depth), (up,),
            (up, width), vector, vector, vector,
        ]
    return pl.pallas_call(
        functools.partial(finish_kernel, fused),
        grid=(TILES,),
        in_specs=[tile, tile] + [resident(a.shape) for a in sums],
        out_specs=[tile] + [pl.BlockSpec(s, lambda i, n=len(s): (0,) * n) for s in shapes[1:]],
        out_shape=[shape_of(s, F32) for s in shapes],
        compiler_params=params(),
        name="finish",
    )(part, d_attn, *sums)


def per_device(
    sizes, tokens, cotangent, groups, qkv_weight, query_bias, value_bias, out_weight, out_bias, gain_one,
    shift_one, up_weight, up_bias, down_weight, down_bias, gain_two, shift_two,
):
    n_wide, n_narrow = sizes
    sents, seq, width = tokens.shape
    depth = up_weight.shape[1]
    rows = sents * seq
    flat = lambda v: v.reshape(rows, v.shape[-1])

    qkv, probs, ctx = attend(tokens, qkv_weight, query_bias, value_bias)
    block_out, low, xh1, rs1, hidden, slope, xh2, rs2, cls, slots = forward(
        tokens, ctx, out_weight, out_bias, gain_one, shift_one, up_weight, up_bias, down_weight, down_bias,
        gain_two, shift_two, sizes,
    )
    gathered = slots.reshape(n_wide * n_narrow * (sents // 2), 2 * width)
    loss, d_down, sums_two = ranking(gathered, groups, cls, cotangent, xh2, rs2, gain_two)
    d_up, d_attn, d_ctx, sums_one, up_sum, out_terms, down_terms = backward(
        d_down, flat(hidden), flat(slope), down_weight, up_weight, flat(xh1), flat(rs1), gain_one, out_weight,
        ctx, sizes,
    )
    part, vectors, *sums = tail(
        flat(low), d_up, qkv, d_ctx, probs, flat(tokens), qkv_weight, out_terms, down_terms, sums_one, sums_two,
        up_sum, sizes,
    )
    if sizes == (16, 2):
        input_grad, *grads = finish(part, d_attn, [*sums, vectors], sizes, depth)
    else:
        (input_grad,) = finish(part, d_attn, [], sizes, depth)
        up_terms, qkv_terms = sums
        quad = width // QUADS
        qkv_terms = qkv_terms.reshape(width, QUADS, 3, quad).transpose(0, 2, 1, 3).reshape(width, 3 * width)
        total = lambda v: lax.psum(
            lax.psum_scatter(v, "wide", scatter_dimension=0, tiled=True).astype(F32), "narrow"
        )
        vector = lambda n: total(vectors[n])
        grads = (
            total(qkv_terms), vector(0), vector(1), total(out_terms), vector(2), vector(3), vector(4),
            total(up_terms), total(vectors[8 : 8 + UPS].reshape(-1)), total(down_terms), vector(5), vector(6),
            vector(7),
        )
    return (loss.reshape(()), block_out, input_grad.reshape(sents, seq, width), *grads)


def solution(mesh):
    sizes = (mesh.shape["wide"], mesh.shape["narrow"])
    split = P(("wide", "narrow"), None, None)
    matrix, vector = P("wide", None), P("wide")
    return jax.shard_map(
        functools.partial(per_device, sizes),
        mesh=mesh,
        in_specs=(split, split) + (P(),) * 14,
        out_specs=(
            P(), split, split, matrix, vector, vector, matrix, vector, vector, vector, matrix, vector,
            matrix, vector, vector, vector,
        ),
        check_vma=False,
    )
```

profile of v0, /device:TPU:0, one launch (start us, length us, event | category | flops | bytes accessed | tf_op | source)
XLA Modules:
  0.0 252.7 jit_solution(10402504569349790886)
XLA Ops:
  0.6 28.1 %attend.1 = (bf16[2048,2304]{1,0:T(8,128)(2,1)}, bf16[32,64,768]{2,1,0:T(8,128)(2,1)}, bf16[2048,768]{1,0:T(8,128)(2,1)}) custom-call(bf16[32,64,768]{2,1,0:T(8,128)(2,1)} %x_ref.3, bf16[768,2304]{1,0:T(8,128)(2,1)} %refs_8_.3, f32[768]{0:T(1024)} %qb_ref.1, f32[768]{0:T(1024)} %vb_ref.1), custom_call_target="tpu_custom_call" | custom-call | tf_op jit(solution)/shard_map/attend/pallas_call | solution.py:108
  28.8 48.8 %forward.1 = (bf16[32,64,768]{2,1,0:T(8,128)(2,1)}, bf16[32,64,768]{2,1,0:T(8,128)(2,1)}, bf16[32,64,768]{2,1,0:T(8,128)(2,1)}, f32[32,64,128]{2,1,0:T(8,128)}, ...) custom-call(bf16[32,64,768]{2,1,0:T(8,128)(2,1)} %x_ref.3, ...), custom_call_target="tpu_custom_call" | custom-call | tf_op jit(solution)/shard_map/forward/pallas_call | solution.py:282
  77.6 12.3 %ranking.1 = (f32[1,1]{1,0:T(1,128)}, bf16[2048,768]{1,0:T(8,128)(2,1)}, f32[8,768]{1,0:T(8,128)}) custom-call(bf16[512,1536]{1,0:T(8,128)(2,1)} %bitcast.16, s32[512]{0:T(512)} %group_ref.1, f32[32,768]{1,0:T(8,128)} %get-tuple-element.61.cls_ref, bf16[32,64,768]{2,1,0:T(8,128)(2,1)} %cot_ref.1, bf16[32,64,768]{2,1,0:T(8,128)(2,1)} %get-tuple-element.62.xh2_ref, ...), custom_call_target="tpu_custom_call" | custom-call | tf_op jit(solution)/shard_map/ranking/pallas_call | solution.py:400
  89.9 58.5 %backward.1 = (bf16[2048,3072]{1,0:T(8,128)(2,1)}, bf16[2048,768]{1,0:T(8,128)(2,1)}, bf16[2048,768]{1,0:T(8,128)(2,1)}, f32[8,768]{1,0:T(8,128)}, f32[1,3072]{1...) custom-call(bf16[2048,768]{1,0:T(8,128)(2,1)} %get-tuple-element.67.refs_0_, ...), custom_call_target="tpu_custom_call" | custom-call | tf_op jit(solution)/shard_map/backward/pallas_call | solution.py:663
  148.5 95.3 %tail.1 = (bf16[2048,768]{1,0:T(8,128)(2,1)}, f32[16,768]{1,0:T(8,128)}, bf16[8,48,384]{2,1,0:T(8,128)(2,1)}, bf16[8,48,384]{2,1,0:T(8,128)(2,1)}, bf16[192,384]{1,0:T(8,128)(2,1)}, /*index=5*/bf16[192,384]{1,0:T(8,128)(2,1)}) custom-call(bf16[2048,768]{1,0:T(8,128)(2,1)} %bitcast.14, bf16[2048,3072]{1,0:T(8,128)(2,1)} %get-tuple-element.72.refs_1_, ...), custom_call_target="tpu_custom_call" | custom-call | tf_op jit(solution)/shard_map/tail/pallas_call | solution.py:945
  243.8 0.0 copy-start
  243.8 7.2 %finish.1 = (f32[2048,768]{1,0:T(8,128)}, f32[48,2304]{1,0:T(8,128)}, f32[48]{0:T(128)}, f32[48]{0:T(128)}, f32[48,768]{1,0:T(8,128)}, /*index=5*/f32[48]{0:T(12...) custom-call(bf16[2048,768]{1,0:T(8,128)(2,1)} %get-tuple-element.81., ...), custom_call_target="tpu_custom_call" | custom-call | tf_op jit(solution)/shard_map/finish/pallas_call | solution.py:1016
  251.0 0.0 copy-done
  251.0 1.7 copy.33
Async XLA Ops:
  243.8 7.2 %copy-start = (bf16[32,64,768]{2,1,0:T(8,128)(2,1)S(1)}, bf16[32,64,768]{2,1,0:T(8,128)(2,1)}, u32[]{:S(2)}) copy-start(bf16[32,64,768]{2,1,0:T(8,128)(2,1)} %get-tuple-element.119) | copy-start | bytes 9437188
where the time goes:
time: 253 us
  Pallas kernels  250 us (99%)
    pallas_call x1, Pallas kernels, tail(): pl.pallas_call(functools.partial(tail_kernel, fused, nz), grid=(STEPS,),...  95.3 us
    pallas_call x1, Pallas kernels, backward(): pl.pallas_call(functools.partial(backward_kernel, fused, nz), grid=(8,),...  58.5 us
    pallas_call x1, Pallas kernels, forward(): pl.pallas_call(forward_kernel, grid=(4,), in_specs=[tile(width), tile(wid...  48.8 us
    pallas_call x1, Pallas kernels, attend(): pl.pallas_call(attend_kernel, grid=(sents // SIDE,), in_specs=[pl.BlockSp...  28.1 us
    pallas_call x1, Pallas kernels, ranking(): pl.pallas_call(ranking_kernel, grid=(sents // SIDE,), in_specs=[resident(...  12.3 us
    pallas_call x1, Pallas kernels, finish(): pl.pallas_call(functools.partial(finish_kernel, fused), grid=(TILES,), in...  7.16 us

commit v1 on v0

--- a/solution.py
+++ b/solution.py
@@ -143,7 +143,7 @@
 
 def forward_kernel(
     x_ref, ctx_ref, ow_ref, ob_ref, g1_ref, s1_ref, uw_hbm, ub_ref, dw_hbm, db_ref, g2_ref, s2_ref,
-    out_ref, low_ref, xh1_ref, rs1_ref, hid_ref, slope_ref, xh2_ref, rs2_ref, cls_ref, all_ref,
+    low_ref, xh1_ref, rs1_ref, hid_ref, slope_ref, xh2_ref, rs2_ref, cls_ref, all_ref,
     rows_ref, uw_ref, dw_ref, w_sems, buf, zs, zr, ys, yr, xs, xr, cs, cr, done,
 ):
     sents, part, width = x_ref.shape
@@ -151,37 +151,34 @@
     rows = sents * part
     step = pl.program_id(0)
     wide, narrow, z, y, core = place()
-    nz, nx = buf.shape[0], buf.shape[3]
+    nz, nx = buf.shape[1], buf.shape[4]
     wide_of = lambda a, b, c: (a * 2 + b) * 2 + c
-
     z_peers = [(lax.rem(z + k, nz), k) for k in range(1, nz)]
     x_peers = [(lax.rem(narrow + k, nx), k) for k in range(1, nx)]
+
+    def gather_copy(slots, sems, at, device):
+        return pltpu.make_async_remote_copy(
+            src_ref=buf.at[slots], dst_ref=buf.at[slots], send_sem=sems[0].at[at], recv_sem=sems[1].at[at],
+            device_id=device, device_id_type=MESH,
+        )
+
+    every = slice(None)
     z_copies = [
-        pltpu.make_async_remote_copy(
-            src_ref=buf.at[z, y, core, narrow], dst_ref=buf.at[z, y, core, narrow],
-            send_sem=zs.at[k - 1], recv_sem=zr.at[k - 1],
-            device_id=(wide_of(to, y, core), narrow), device_id_type=MESH,
-        )
+        gather_copy((every, z, y, core, narrow), (zs, zr), k - 1, (wide_of(to, y, core), narrow))
         for to, k in z_peers
     ]
-    y_copy = pltpu.make_async_remote_copy(
-        src_ref=buf.at[:, y, core, narrow], dst_ref=buf.at[:, y, core, narrow],
-        send_sem=ys, recv_sem=yr,
-        device_id=(wide_of(z, 1 - y, core), narrow), device_id_type=MESH,
-    )
-    x_copies = [
-        pltpu.make_async_remote_copy(
-            src_ref=buf.at[:, :, core, narrow], dst_ref=buf.at[:, :, core, narrow],
-            send_sem=xs.at[k - 1], recv_sem=xr.at[k - 1],
-            device_id=(wide, to), device_id_type=MESH,
-        )
-        for to, k in x_peers
-    ]
-    core_copy = pltpu.make_async_remote_copy(
-        src_ref=buf.at[:, :, core], dst_ref=buf.at[:, :, core],
-        send_sem=cs, recv_sem=cr,
-        device_id=(wide_of(z, y, 1 - core), narrow), device_id_type=MESH,
-    )
+
+    def over_y(half, xs_held, at):
+        return gather_copy((half, every, y, core, xs_held), (ys, yr), at, (wide_of(z, 1 - y, core), narrow))
+
+    def over_x(half, ys_held, first):
+        return [
+            gather_copy((half, every, ys_held, core, narrow), (xs, xr), first + k - 1, (wide, to)) for to, k in x_peers
+        ]
+
+    second = [over_y(0, narrow, 0), *over_x(1, y, 0)]
+    third = [*over_x(0, every, nx - 1), over_y(1, every, 1)]
+    core_copy = gather_copy((every, every, every, core), (cs, cr), 0, (wide_of(z, y, 1 - core), narrow))
 
     barrier = pltpu.get_barrier_semaphore()
     weights = [
@@ -198,7 +195,6 @@
         for to, _ in x_peers:
             pl.semaphore_signal(barrier, inc=1, device_id=(wide, to), device_id_type=MESH)
         pl.semaphore_signal(barrier, inc=1, device_id=(wide_of(z, y, 1 - core), narrow), device_id_type=MESH)
-        pl.semaphore_wait(barrier, nz + nx)
 
     block = lambda ref: ref[...].reshape(rows, ref.shape[2])
 
@@ -220,6 +216,25 @@
             copy.wait()
 
     for c in range(depth // width):
+        if c == 2:
+
+            @pl.when(step == 0)
+            def _():
+                pl.semaphore_wait(barrier, nz + nx)
+
+            @pl.when(step == 2)
+            def _():
+                for copy in second:
+                    copy.wait()
+                for copy in third:
+                    copy.start()
+
+            @pl.when(step == 3)
+            def _():
+                for copy in third:
+                    copy.wait()
+                core_copy.start()
+
         cols = slice(c * width, (c + 1) * width)
         up = nn(low, uw_ref[:, cols]) + ub_ref[cols].reshape(1, width)
         cdf = 0.5 * (lax.erf(up * 0.7071067811865476) + 1.0)
@@ -230,7 +245,6 @@
         total = total + nn(hidden, dw_ref[cols, :])
     xh2, rs2 = norm(total)
     final = xh2 * line(g2_ref) + line(s2_ref)
-    put(out_ref, final)
     put(xh2_ref, xh2)
     put(rs2_ref, jnp.broadcast_to(rs2, (rows, 128)))
 
@@ -241,9 +255,9 @@
         cls = cls_ref[...]
         pooled = cls * lax.rsqrt(jnp.sum(cls * cls, -1, keepdims=True) + EPS)
         for s in range(sents):
-            half = slice(s % 2 * width, (s % 2 + 1) * width)
-            rows_ref[s // 2 : s // 2 + 1, half] = pooled[s : s + 1, :]
-        buf[z, y, core, narrow] = rows_ref[...].astype(BF)
+            rows_ref[s % 2, s // 2 : s // 2 + 1, :] = pooled[s : s + 1, :]
+        for half in range(2):
+            buf[half, z, y, core, narrow] = rows_ref[half].astype(BF)
         for copy in z_copies:
             copy.start()
 
@@ -251,19 +265,11 @@
     def _():
         for copy in z_copies:
             copy.wait()
-        y_copy.start()
-
-    @pl.when(step == 2)
-    def _():
-        y_copy.wait()
-        for copy in x_copies:
+        for copy in second:
             copy.start()
 
     @pl.when(step == 3)
     def _():
-        for copy in x_copies:
-            copy.wait()
-        core_copy.start()
         core_copy.wait()
         out = pltpu.make_async_copy(buf, all_ref, done)
         out.start()
@@ -277,7 +283,7 @@
     nz, nx = sizes[0] // 4, sizes[1]
     tile = lambda lanes: pl.BlockSpec((sents, part, lanes), lambda i: (0, i, 0))
     whole = lambda lanes, dtype: shape_of((sents, seq, lanes), dtype)
-    slots = (nz, 2, 2, nx, sents // 2, 2 * width)
+    slots = (2, nz, 2, 2, nx, sents // 2, width)
     dma = pltpu.SemaphoreType.DMA
     return pl.pallas_call(
         forward_kernel,
@@ -289,18 +295,19 @@
             resident(db.shape), resident(g2.shape), resident(s2.shape),
         ],
         out_specs=[
-            tile(width), tile(width), tile(width), tile(128), tile(depth), tile(depth), tile(width),
+            tile(width), tile(width), tile(128), tile(depth), tile(depth), tile(width),
             tile(128), pl.BlockSpec((sents, width), lambda i: (0, 0)), pl.BlockSpec(memory_space=pl.ANY),
         ],
         out_shape=[
-            whole(width, BF), whole(width, BF), whole(width, BF), whole(128, F32), whole(depth, BF),
+            whole(width, BF), whole(width, BF), whole(128, F32), whole(depth, BF),
             whole(depth, BF), whole(width, BF), whole(128, F32), shape_of((sents, width), F32),
             shape_of(slots, BF),
         ],
         scratch_shapes=[
-            pltpu.VMEM((sents // 2, 2 * width), F32), pltpu.VMEM(uw.shape, BF), pltpu.VMEM(dw.shape, BF), dma((2,)),
+            pltpu.VMEM((2, sents // 2, width), F32), pltpu.VMEM(uw.shape, BF), pltpu.VMEM(dw.shape, BF), dma((2,)),
             pltpu.VMEM(slots, BF),
-            dma((nz - 1,)), dma((nz - 1,)), dma, dma, dma((nx - 1,)), dma((nx - 1,)), dma, dma, dma,
+            dma((nz - 1,)), dma((nz - 1,)), dma((2,)), dma((2,)), dma((2 * nx - 2,)), dma((2 * nx - 2,)), dma((1,)),
+            dma((1,)), dma,
         ],
         compiler_params=params(collective_id=0, has_side_effects=True),
         name="forward",
@@ -308,10 +315,10 @@
 
 
 def ranking_kernel(
-    all_ref, group_ref, cls_ref, cot_ref, xh2_ref, rs2_ref, g2_ref,
-    loss_ref, down_ref, sums_ref, dcls, gcol_ref,
+    all_ref, group_ref, cls_ref, cot_ref, xh2_ref, rs2_ref, g2_ref, s2_ref,
+    loss_ref, out_ref, down_ref, sums_ref, dcls, gcol_ref,
 ):
-    pairs, width = all_ref.shape[0], all_ref.shape[1] // 2
+    _, pairs, width = all_ref.shape
     own = cls_ref.shape[0] // 2
     step = pl.program_id(0)
 
@@ -331,12 +338,12 @@
             return nt(left, right) * SCALE - jnp.where(hit, SCALE * MARGIN, 0.0), hit
 
         def column_lse(left_at, right_at):
-            right = all_ref[:, right_at * width : (right_at + 1) * width]
+            right = all_ref[right_at]
 
             def strip_step(at, carry):
                 top, total, diag = carry
                 start = pl.multiple_of(at * strip, strip)
-                left = all_ref[pl.ds(start, strip), left_at * width : (left_at + 1) * width]
+                left = all_ref[left_at, pl.ds(start, strip), :]
                 logits, hit = logits_of(left, right, start)
                 masked = jnp.where(gcol_ref[pl.ds(start, strip), :1] == groups, logits, -1e30)
                 peak = jnp.maximum(top, jnp.max(masked, axis=0, keepdims=True))
@@ -355,8 +362,8 @@
         same = gcol_ref[own_rows, :1] == groups
 
         def side(my_at, other_at, other_lse):
-            other = all_ref[:, other_at * width : (other_at + 1) * width]
-            mine = all_ref[own_rows, my_at * width : (my_at + 1) * width]
+            other = all_ref[other_at]
+            mine = all_ref[my_at, own_rows, :]
             logits, hit = logits_of(mine, other, first)
             eye = hit.astype(F32)
             masked = jnp.where(same, logits, -1e30)
@@ -384,6 +391,7 @@
     d_final = d_final.reshape(rows, width)
     xhat = xh2_ref[...].reshape(rows, width).astype(F32)
     root = rs2_ref[...].reshape(rows, 128)[:, :1]
+    out_ref[...] = (xhat * line(g2_ref) + line(s2_ref)).astype(BF).reshape(out_ref.shape)
     e = d_final * line(g2_ref)
     d_pre = (e - jnp.mean(e, -1, keepdims=True) - xhat * jnp.mean(e * xhat, -1, keepdims=True)) * root
     d_down = d_pre.astype(BF)
@@ -393,27 +401,27 @@
     sums_ref[2:3, :] += jnp.sum(d_down.astype(F32), axis=0, keepdims=True)
 
 
-def ranking(gathered, groups, cls, cotangent, xh2, rs2, g2):
+def ranking(gathered, groups, cls, cotangent, xh2, rs2, g2, s2):
     sents, seq, width = cotangent.shape
-    pairs = gathered.shape[0]
+    pairs = gathered.shape[1]
     tile = lambda lanes: pl.BlockSpec((SIDE, seq, lanes), lambda i: (i, 0, 0))
     return pl.pallas_call(
         ranking_kernel,
         grid=(sents // SIDE,),
         in_specs=[
             resident(gathered.shape), resident(groups.shape), resident(cls.shape), tile(width), tile(width), tile(128),
-            resident(g2.shape),
+            resident(g2.shape), resident(s2.shape),
         ],
         out_specs=[
-            pl.BlockSpec((1, 1), lambda i: (0, 0)),
+            pl.BlockSpec((1, 1), lambda i: (0, 0)), tile(width),
             pl.BlockSpec((SIDE * seq, width), lambda i: (i, 0)),
             pl.BlockSpec((8, width), lambda i: (0, 0)),
         ],
-        out_shape=[shape_of((1, 1), F32), shape_of((sents * seq, width), BF), shape_of((8, width), F32)],
+        out_shape=[shape_of((1, 1), F32), shape_of(cotangent.shape, BF), shape_of((sents * seq, width), BF), shape_of((8, width), F32)],
         scratch_shapes=[pltpu.VMEM((sents, width), F32), pltpu.VMEM((pairs, 128), jnp.int32)],
         compiler_params=params(),
         name="ranking",
-    )(gathered, groups, cls, cotangent, xh2, rs2, g2)
+    )(gathered, groups, cls, cotangent, xh2, rs2, g2, s2)
 
 
 def copy_to(src, dst, sends, recvs, at, device):
@@ -424,6 +432,8 @@
 
 
 def plus(*terms):
+    if len(terms) == 2:
+        return terms[0] + terms[1]
     return sum(t.astype(F32) for t in terms).astype(BF)
 
 
@@ -441,7 +451,9 @@
         barrier = pltpu.get_barrier_semaphore()
         for device in devices:
             pl.semaphore_signal(barrier, inc=1, device_id=device, device_id_type=MESH)
-        pl.semaphore_wait(barrier, len(devices))
+
+    def met(self, count):
+        pl.semaphore_wait(pltpu.get_barrier_semaphore(), count)
 
 
 class Stages:
@@ -449,44 +461,52 @@
 
     def __init__(self, peers, terms, got, sends, recvs):
         self.peers, self.terms, self.got, self.sends, self.recvs = peers, terms, got, sends, recvs
-        self.third = got["xa"].shape[2]
+        self.half = peers.nz // 2
 
     @staticmethod
     def scratch(nz, rows, cols):
-        third = rows // 3
+        half = nz // 2
         return {
-            "xa": (nz, 2, third, cols), "yb": (2, nz, rows - third, cols),
-            "ya": (nz, third, cols), "xb": (nz, rows - third, cols),
+            "xa": (half, 2, rows, cols), "yb": (2, nz - half, rows, cols), "ya": (half, rows, cols),
+            "xb": (nz - half, rows, cols),
         }
 
+    def first_of(self, z, at):
+        p = self.peers
+        if z < self.half:
+            return copy_to(self.terms.at[1 - p.x, z], self.got["xa"].at[z], self.sends, self.recvs, at, p.over_x)
+        return copy_to(
+            self.terms.at[:, z, 1 - p.y], self.got["yb"].at[:, z - self.half], self.sends, self.recvs, at, p.over_y
+        )
+
     def first(self):
-        p, t = self.peers, self.third
+        p, h = self.peers, self.half
         return [
-            copy_to(self.terms.at[1 - p.x, :, :, :t], self.got["xa"], self.sends, self.recvs, 1, p.over_x),
-            copy_to(self.terms.at[:, :, 1 - p.y, t:], self.got["yb"], self.sends, self.recvs, 2, p.over_y),
+            copy_to(self.terms.at[1 - p.x, :h], self.got["xa"], self.sends, self.recvs, 1, p.over_x),
+            copy_to(self.terms.at[:, h:, 1 - p.y], self.got["yb"], self.sends, self.recvs, 2, p.over_y),
         ]
 
     def second(self):
-        p, t = self.peers, self.third
+        p, h = self.peers, self.half
         return [
-            copy_to(self.terms.at[p.x, :, 1 - p.y, :t], self.got["ya"], self.sends, self.recvs, 3, p.over_y),
-            copy_to(self.terms.at[1 - p.x, :, p.y, t:], self.got["xb"], self.sends, self.recvs, 4, p.over_x),
+            copy_to(self.terms.at[p.x, :h, 1 - p.y], self.got["ya"], self.sends, self.recvs, 3, p.over_y),
+            copy_to(self.terms.at[1 - p.x, h:, p.y], self.got["xb"], self.sends, self.recvs, 4, p.over_x),
         ]
 
-    def add_first(self):
-        p, t = self.peers, self.third
-        for copy in self.first():
+    def add_first(self, copies=None):
+        p, h = self.peers, self.half
+        for copy in copies or self.first():
             copy.wait()
-        self.terms[p.x, :, :, :t] = plus(self.terms[p.x, :, :, :t], self.got["xa"][...])
-        for h in range(2):
-            self.terms[h, :, p.y, t:] = plus(self.terms[h, :, p.y, t:], self.got["yb"][h])
+        self.terms[p.x, :h] = plus(self.terms[p.x, :h], self.got["xa"][...])
+        for x in range(2):
+            self.terms[x, h:, p.y] = plus(self.terms[x, h:, p.y], self.got["yb"][x])
 
     def add_second(self):
-        p, t = self.peers, self.third
+        p, h = self.peers, self.half
         for copy in self.second():
             copy.wait()
-        self.terms[p.x, :, p.y, :t] = plus(self.terms[p.x, :, p.y, :t], self.got["ya"][...])
-        self.terms[p.x, :, p.y, t:] = plus(self.terms[p.x, :, p.y, t:], self.got["xb"][...])
+        self.terms[p.x, :h, p.y] = plus(self.terms[p.x, :h, p.y], self.got["ya"][...])
+        self.terms[p.x, h:, p.y] = plus(self.terms[p.x, h:, p.y], self.got["xb"][...])
 
 
 class Finish:
@@ -556,11 +576,22 @@
         exchange(i).wait()
         for h in range(2):
             terms[h, i] = plus(terms[h, i], got[i % 2, h, 0])
+        for z in range(blocks):
+            if isinstance(i, int) and z != i:
+                continue
+
+            @pl.when(i == z)
+            def _(z=z):
+                stages.first_of(z, Stages.SEMS + z).start()
 
     @pl.when(step < blocks)
     def _():
         value = tn(hid_ref[...], down_ref[...])
         if fused:
+
+            @pl.when(step == 0)
+            def _():
+                peers.met(3)
 
             @pl.when(step > 0)
             def _():
@@ -613,12 +644,10 @@
         @pl.when(step == blocks)
         def _():
             settle(blocks - 1)
-            for copy in stages.first():
-                copy.start()
-
-        @pl.when(step == blocks + 2)
-        def _():
-            stages.add_first()
+
+        @pl.when(step == blocks + 1)
+        def _():
+            stages.add_first([stages.first_of(z, Stages.SEMS + z) for z in range(blocks)])
             for copy in stages.second():
                 copy.start()
 
@@ -652,7 +681,7 @@
             pltpu.VMEM((2, 2, 1, 2, shard, half), BF),
         ]
         scratch += [pltpu.VMEM(s, BF) for s in Stages.scratch(nz, shard, half).values()]
-        scratch += [dma((4,)), dma((4,)), dma((Stages.SEMS,)), dma((Stages.SEMS,))]
+        scratch += [dma((4,)), dma((4,)), dma((Stages.SEMS + 4,)), dma((Stages.SEMS + 4,))]
         dwg_spec, dwg_shape = once(nz, shard, half), (nz, shard, half)
         owg_shape = (2, 2, nz, 2, width // sizes[0], half)
         extra = dict(collective_id=1, has_side_effects=True)
@@ -686,7 +715,7 @@
 FIRST_QUAD = UPS
 FIRST_INPUT = UPS + QUADS * TILES
 STEPS = FIRST_INPUT + TILES
-OUT_PIECE, UP_PIECE, QUAD_PIECE = 0, 1, 1 + UPS
+UP_PIECE, OUT_PIECE, QUAD_PIECE = 0, UPS, 1 + UPS
 PIECES = UPS + 1 + QUADS
 VECTORS = 16
 
@@ -755,7 +784,7 @@
             finish_of(n).along_x().wait()
 
         usual, hurried = (1, 3, 5, 7, 8), (1, 2, 3, 4, STEPS)
-        ready = [*range(-1, UPS)] + [FIRST_QUAD + TILES * (q + 1) - 1 for q in range(QUADS)]
+        ready = [*range(UPS + 1)] + [FIRST_QUAD + TILES * (q + 1) - 1 for q in range(QUADS)]
 
         def settle():
             for stage, action in enumerate((add_chip, add_first, add_second, add_z, last)):
@@ -777,12 +806,6 @@
         @pl.when(step == 0)
         def _():
             peers.greet([peers.sibling, peers.over_x, peers.over_y, *peers.over_z])
-            for copy in down.along_z():
-                copy.start()
-            for h in range(2):
-                terms[OUT_PIECE, h] = owg_ref[0, h]
-                send[OUT_PIECE, h] = owg_ref[1, h]
-            chip(OUT_PIECE).start()
 
     @pl.when(step == 0)
     def _():
@@ -839,7 +862,22 @@
             acc[...] += part
 
     if fused:
+
+        @pl.when(step == 0)
+        def _():
+            peers.met(2 + nz)
+            for copy in down.along_z():
+                copy.start()
+
         settle()
+
+        @pl.when(step == UPS)
+        def _():
+            for h in range(2):
+                terms[OUT_PIECE, h] = owg_ref[0, h]
+                send[OUT_PIECE % 2, h] = owg_ref[1, h]
+            chip(OUT_PIECE).start()
+
         done_quad = (step >= FIRST_QUAD) & (step < FIRST_INPUT) & (tile == TILES - 1)
 
         @pl.when((step < UPS) | done_quad)
@@ -1035,12 +1073,14 @@
     flat = lambda v: v.reshape(rows, v.shape[-1])
 
     qkv, probs, ctx = attend(tokens, qkv_weight, query_bias, value_bias)
-    block_out, low, xh1, rs1, hidden, slope, xh2, rs2, cls, slots = forward(
+    low, xh1, rs1, hidden, slope, xh2, rs2, cls, slots = forward(
         tokens, ctx, out_weight, out_bias, gain_one, shift_one, up_weight, up_bias, down_weight, down_bias,
         gain_two, shift_two, sizes,
     )
-    gathered = slots.reshape(n_wide * n_narrow * (sents // 2), 2 * width)
-    loss, d_down, sums_two = ranking(gathered, groups, cls, cotangent, xh2, rs2, gain_two)
+    gathered = slots.reshape(2, n_wide * n_narrow * (sents // 2), width)
+    loss, block_out, d_down, sums_two = ranking(
+        gathered, groups, cls, cotangent, xh2, rs2, gain_two, shift_two
+    )
     d_up, d_attn, d_ctx, sums_one, up_sum, out_terms, down_terms = backward(
         d_down, flat(hidden), flat(slope), down_weight, up_weight, flat(xh1), flat(rs1), gain_one, out_weight,
         ctx, sizes,

time: 253 us -> 237 us (0.937)
  Pallas kernels: 250 us -> 236 us
    pallas_call x1, Pallas kernels: 58.5 us -> 51.5 us  [backward(): pl.pallas_call(functools.partial(backward_kernel, fused, nz), grid=(8,),...]
    pallas_call x1, Pallas kernels: 48.8 us -> 44.3 us  [forward(): pl.pallas_call(forward_kernel, grid=(4,), in_specs=[tile(width), tile(wid...]
    pallas_call x1, Pallas kernels: 95.3 us -> 91.9 us  [tail(): pl.pallas_call(functools.partial(tail_kernel, fused, nz), grid=(STEPS,),...]
where the time goes in v1:
time: 237 us; the launch traced here: 236 us
  Pallas kernels  236 us (100%)
    pallas_call x1, Pallas kernels, tail(): pl.pallas_call(functools.partial(tail_kernel, fused, nz), grid=(STEPS,),...  91.9 us
    pallas_call x1, Pallas kernels, backward(): pl.pallas_call(functools.partial(backward_kernel, fused, nz), grid=(8,),...  51.5 us
    pallas_call x1, Pallas kernels, forward(): pl.pallas_call(forward_kernel, grid=(4,), in_specs=[tile(width), tile(wid...  44.3 us
    pallas_call x1, Pallas kernels, attend(): pl.pallas_call(attend_kernel, grid=(sents // SIDE,), in_specs=[pl.BlockSp...  28.2 us
    pallas_call x1, Pallas kernels, ranking(): pl.pallas_call(ranking_kernel, grid=(sents // SIDE,), in_specs=[resident(...  12.8 us
    pallas_call x1, Pallas kernels, finish(): pl.pallas_call(functools.partial(finish_kernel, fused), grid=(TILES,), in...  7.01 us

profile of v1, /device:TPU:0, one launch (start us, length us, event | category | flops | bytes accessed | tf_op | source)
XLA Modules:
  0.0 236.5 jit_solution(11386705330204072164)
XLA Ops:
  0.6 28.2 %attend.1 = (bf16[2048,2304]{1,0:T(8,128)(2,1)}, bf16[32,64,768]{2,1,0:T(8,128)(2,1)}, bf16[2048,768]{1,0:T(8,128)(2,1)}) custom-call(bf16[32,64,768]{2,1,0:T(8,128)(2,1)} %x_ref.3, bf16[768,2304]{1,0:T(8,128)(2,1)} %refs_8_.3, f32[768]{0:T(1024)} %qb_ref.1, f32[768]{0:T(1024)} %vb_ref.1), custom_call_target="tpu_custom_call" | custom-call | tf_op jit(solution)/shard_map/attend/pallas_call | solution.py:108
  28.8 44.3 %forward.1 = (bf16[32,64,768]{2,1,0:T(8,128)(2,1)}, bf16[32,64,768]{2,1,0:T(8,128)(2,1)}, f32[32,64,128]{2,1,0:T(8,128)}, bf16[32,64,3072]{2,1,0:T(8,128)(2,1)},...) custom-call(bf16[32,64,768]{2,1,0:T(8,128)(2,1)} %x_ref.3, ...), custom_call_target="tpu_custom_call" | custom-call | tf_op jit(solution)/shard_map/forward/pallas_call | solution.py:288
  73.1 12.8 %ranking.1 = (f32[1,1]{1,0:T(1,128)}, bf16[32,64,768]{2,1,0:T(8,128)(2,1)}, bf16[2048,768]{1,0:T(8,128)(2,1)}, f32[8,768]{1,0:T(8,128)}) custom-call(bf16[2,512,768]{2,1,0:T(8,128)(2,1)} %bitcast.16, s32[512]{0:T(512)} %group_ref.1, f32[32,768]{1,0:T(8,128)} %get-tuple-element.61.cls_ref, bf16[32,64,768]{2,1,0:T(8,128)(2,1)} %cot_ref.1, ...), custom_call_target="tpu_custom_call" | custom-call | tf_op jit(solution)/shard_map/ranking/pallas_call | solution.py:408
  85.9 51.5 %backward.1 = (bf16[2048,3072]{1,0:T(8,128)(2,1)}, bf16[2048,768]{1,0:T(8,128)(2,1)}, bf16[2048,768]{1,0:T(8,128)(2,1)}, f32[8,768]{1,0:T(8,128)}, f32[1,3072]{1...) custom-call(bf16[2048,768]{1,0:T(8,128)(2,1)} %get-tuple-element.67.refs_0_, ...), custom_call_target="tpu_custom_call" | custom-call | tf_op jit(solution)/shard_map/backward/pallas_call | solution.py:692
  137.4 91.9 %tail.1 = (bf16[2048,768]{1,0:T(8,128)(2,1)}, f32[16,768]{1,0:T(8,128)}, bf16[8,48,384]{2,1,0:T(8,128)(2,1)}, bf16[8,48,384]{2,1,0:T(8,128)(2,1)}, bf16[192,384]{1,0:T(8,128)(2,1)}, /*index=5*/bf16[192,384]{1,0:T(8,128)(2,1)}) custom-call(bf16[2048,768]{1,0:T(8,128)(2,1)} %bitcast.14, bf16[2048,3072]{1,0:T(8,128)(2,1)} %get-tuple-element.72.refs_1_, ...), custom_call_target="tpu_custom_call" | custom-call | tf_op jit(solution)/shard_map/tail/pallas_call | solution.py:983
  229.3 7.0 %finish.1 = (f32[2048,768]{1,0:T(8,128)}, f32[48,2304]{1,0:T(8,128)}, f32[48]{0:T(128)}, f32[48]{0:T(128)}, f32[48,768]{1,0:T(8,128)}, /*index=5*/f32[48]{0:T(12...) custom-call(bf16[2048,768]{1,0:T(8,128)(2,1)} %get-tuple-element.81., ...), custom_call_target="tpu_custom_call" | custom-call | tf_op jit(solution)/shard_map/finish/pallas_call | solution.py:1054

commit v2 on v1

--- a/solution.py
+++ b/solution.py
@@ -88,17 +88,21 @@
         qkv_ref[:, cols] = y.astype(BF)
     mask = head_mask(quad)
     scale = (width // HEADS) ** -0.5
-    for s in range(sents):
-        at = slice(s * seq, (s + 1) * seq)
-        for g in range(width // quad):
-            q = qkv_ref[at, g * quad : (g + 1) * quad]
-            k = qkv_ref[at, width + g * quad : width + (g + 1) * quad]
-            v = qkv_ref[at, 2 * width + g * quad : 2 * width + (g + 1) * quad]
-            scores = nt(k, blocked(q, mask)) * scale
-            e = jnp.exp(scores - jnp.max(scores, axis=0, keepdims=True))
-            p = (e * (1.0 / jnp.sum(e, axis=0, keepdims=True))).astype(BF)
-            p_ref[s, :, g * quad : (g + 1) * quad] = p
-            ctx_ref[at, g * quad : (g + 1) * quad] = diagonal(tn(p, v), seq).astype(BF)
+    units = [(s, g) for s in range(sents) for g in range(width // quad)]
+    for first in range(0, len(units), 12):
+        some = units[first : first + 12]
+        rows_of = lambda s: slice(s * seq, (s + 1) * seq)
+        cols_of = lambda g, part: slice(part * width + g * quad, part * width + (g + 1) * quad)
+        scores = [
+            nt(qkv_ref[rows_of(s), cols_of(g, 1)], blocked(qkv_ref[rows_of(s), cols_of(g, 0)], mask)) * scale
+            for s, g in some
+        ]
+        e = [jnp.exp(v - jnp.max(v, axis=0, keepdims=True)) for v in scores]
+        p = [(v * (1.0 / jnp.sum(v, axis=0, keepdims=True))).astype(BF) for v in e]
+        for (s, g), low in zip(some, p, strict=True):
+            p_ref[s, :, cols_of(g, 0)] = low
+            v = qkv_ref[rows_of(s), cols_of(g, 2)]
+            ctx_ref[rows_of(s), cols_of(g, 0)] = diagonal(tn(low, v), seq).astype(BF)
 
 
 def attend(tokens, qkv_weight, query_bias, value_bias):
@@ -831,18 +835,28 @@
         mask = head_mask(quad)
         scale = (quad // QUAD) ** -0.5
         here = lambda size, s=0: pl.ds(pl.multiple_of(tile * rows + s * seq, seq), size)
-        for s in range(sents):
-            at = slice(s * seq, (s + 1) * seq)
-            k = k_ref[at, :]
-            p_low = p_ref[s]
-            p = p_low.astype(F32)
-            dctx = blocked(dctx_ref[at, :], mask)
-            d_probs = nt(v_ref[at, :], dctx)
-            d_scores = (p * (d_probs - jnp.sum(p * d_probs, axis=0, keepdims=True))).astype(BF)
-            dqkv[g, here(seq, s), :quad] = (paired(d_scores, k, seq) * scale).astype(BF)
-            dqkv[g, here(seq, s), quad : 2 * quad] = (nn(d_scores, blocked(q_ref[at, :], mask)) * scale).astype(BF)
-            dqkv[g, here(seq, s), 2 * quad :] = nn(p_low, dctx).astype(BF)
-        grads = dqkv[g, here(rows), :]
+        def sentences(which):
+            k = [k_ref[s * seq : (s + 1) * seq, :] for s in which]
+            low = [p_ref[s] for s in which]
+            p = [v.astype(F32) for v in low]
+            dctx = [blocked(dctx_ref[s * seq : (s + 1) * seq, :], mask) for s in which]
+            d_probs = [nt(v_ref[s * seq : (s + 1) * seq, :], c) for s, c in zip(which, dctx, strict=True)]
+            d_scores = [
+                (a * (b - jnp.sum(a * b, axis=0, keepdims=True))).astype(BF) for a, b in zip(p, d_probs, strict=True)
+            ]
+            d_value = [nn(a, b).astype(BF) for a, b in zip(low, dctx, strict=True)]
+            d_query = [(paired(a, b, seq) * scale).astype(BF) for a, b in zip(d_scores, k, strict=True)]
+            d_key = [
+                (nn(a, blocked(q_ref[s * seq : (s + 1) * seq, :], mask)) * scale).astype(BF)
+                for s, a in zip(which, d_scores, strict=True)
+            ]
+            out = []
+            for s, *three in zip(which, d_query, d_key, d_value, strict=True):
+                out.append(jnp.concatenate(three, axis=1))
+                dqkv[g, here(seq, s), :] = out[-1]
+            return out
+
+        grads = jnp.concatenate(sentences(range(sents)), axis=0)
         part = tn(x_ref[...], grads)
         q_sum = jnp.sum(grads[:, :quad].astype(F32), axis=0, keepdims=True)
         v_sum = jnp.sum(grads[:, 2 * quad :].astype(F32), axis=0, keepdims=True)

time: 237 us -> 222 us (0.937)
  Pallas kernels: 236 us -> 221 us
    pallas_call x1, Pallas kernels: 28.2 us -> 18.7 us  [attend(): pl.pallas_call(attend_kernel, grid=(sents // SIDE,), in_specs=[pl.BlockSp...]
    pallas_call x1, Pallas kernels: 91.9 us -> 86.2 us  [tail(): pl.pallas_call(functools.partial(tail_kernel, fused, nz), grid=(STEPS,),...]
where the time goes in v2:
time: 222 us; the launch traced here: 221 us
  Pallas kernels  221 us (100%)
    pallas_call x1, Pallas kernels, tail(): pl.pallas_call(functools.partial(tail_kernel, fused, nz), grid=(STEPS,),...  86.2 us
    pallas_call x1, Pallas kernels, backward(): pl.pallas_call(functools.partial(backward_kernel, fused, nz), grid=(8,),...  51.4 us
    pallas_call x1, Pallas kernels, forward(): pl.pallas_call(forward_kernel, grid=(4,), in_specs=[tile(width), tile(wid...  44.3 us
    pallas_call x1, Pallas kernels, attend(): pl.pallas_call(attend_kernel, grid=(sents // SIDE,), in_specs=[pl.BlockSp...  18.7 us
    pallas_call x1, Pallas kernels, ranking(): pl.pallas_call(ranking_kernel, grid=(sents // SIDE,), in_specs=[resident(...  12.8 us
    pallas_call x1, Pallas kernels, finish(): pl.pallas_call(functools.partial(finish_kernel, fused), grid=(TILES,), in...  7.01 us

profile of v2, /device:TPU:0, one launch (start us, length us, event | category | flops | bytes accessed | tf_op | source)
XLA Modules:
  0.0 221.4 jit_solution(16129740587841563649)
XLA Ops:
  0.6 18.7 %attend.1 = (bf16[2048,2304]{1,0:T(8,128)(2,1)}, bf16[32,64,768]{2,1,0:T(8,128)(2,1)}, bf16[2048,768]{1,0:T(8,128)(2,1)}) custom-call(bf16[32,64,768]{2,1,0:T(8,128)(2,1)} %x_ref.3, bf16[768,2304]{1,0:T(8,128)(2,1)} %refs_8_.3, f32[768]{0:T(1024)} %qb_ref.1, f32[768]{0:T(1024)} %vb_ref.1), custom_call_target="tpu_custom_call" | custom-call | tf_op jit(solution)/shard_map/attend/pallas_call | solution.py:112
  19.4 44.3 %forward.1 = (bf16[32,64,768]{2,1,0:T(8,128)(2,1)}, bf16[32,64,768]{2,1,0:T(8,128)(2,1)}, f32[32,64,128]{2,1,0:T(8,128)}, bf16[32,64,3072]{2,1,0:T(8,128)(2,1)},...) custom-call(bf16[32,64,768]{2,1,0:T(8,128)(2,1)} %x_ref.3, ...), custom_call_target="tpu_custom_call" | custom-call | tf_op jit(solution)/shard_map/forward/pallas_call | solution.py:292
  63.7 12.8 %ranking.1 = (f32[1,1]{1,0:T(1,128)}, bf16[32,64,768]{2,1,0:T(8,128)(2,1)}, bf16[2048,768]{1,0:T(8,128)(2,1)}, f32[8,768]{1,0:T(8,128)}) custom-call(bf16[2,512,768]{2,1,0:T(8,128)(2,1)} %bitcast.16, s32[512]{0:T(512)} %group_ref.1, f32[32,768]{1,0:T(8,128)} %get-tuple-element.61.cls_ref, bf16[32,64,768]{2,1,0:T(8,128)(2,1)} %cot_ref.1, ...), custom_call_target="tpu_custom_call" | custom-call | tf_op jit(solution)/shard_map/ranking/pallas_call | solution.py:412
  76.5 51.4 %backward.1 = (bf16[2048,3072]{1,0:T(8,128)(2,1)}, bf16[2048,768]{1,0:T(8,128)(2,1)}, bf16[2048,768]{1,0:T(8,128)(2,1)}, f32[8,768]{1,0:T(8,128)}, f32[1,3072]{1...) custom-call(bf16[2048,768]{1,0:T(8,128)(2,1)} %get-tuple-element.67.refs_0_, ...), custom_call_target="tpu_custom_call" | custom-call | tf_op jit(solution)/shard_map/backward/pallas_call | solution.py:696
  128.0 86.2 %tail.1 = (bf16[2048,768]{1,0:T(8,128)(2,1)}, f32[16,768]{1,0:T(8,128)}, bf16[8,48,384]{2,1,0:T(8,128)(2,1)}, bf16[8,48,384]{2,1,0:T(8,128)(2,1)}, bf16[192,384]{1,0:T(8,128)(2,1)}, /*index=5*/bf16[192,384]{1,0:T(8,128)(2,1)}) custom-call(bf16[2048,768]{1,0:T(8,128)(2,1)} %bitcast.14, bf16[2048,3072]{1,0:T(8,128)(2,1)} %get-tuple-element.72.refs_1_, ...), custom_call_target="tpu_custom_call" | custom-call | tf_op jit(solution)/shard_map/tail/pallas_call | solution.py:997
  214.2 7.0 %finish.1 = (f32[2048,768]{1,0:T(8,128)}, f32[48,2304]{1,0:T(8,128)}, f32[48]{0:T(128)}, f32[48]{0:T(128)}, f32[48,768]{1,0:T(8,128)}, /*index=5*/f32[48]{0:T(12...) custom-call(bf16[2048,768]{1,0:T(8,128)(2,1)} %get-tuple-element.81., ...), custom_call_target="tpu_custom_call" | custom-call | tf_op jit(solution)/shard_map/finish/pallas_call | solution.py:1068

commit v3 on v2

--- a/solution.py
+++ b/solution.py
@@ -205,8 +205,17 @@
     def put(ref, value):
         ref[...] = value.astype(ref.dtype).reshape(ref.shape)
 
-    pre_one = block(x_ref).astype(F32) + nn(block(ctx_ref), ow_ref[...]) + line(ob_ref)
-    xh1, rs1 = norm(pre_one)
+    x, ctx = block(x_ref), block(ctx_ref)
+    some = rows // 4
+    cuts = [slice(i * some, (i + 1) * some) for i in range(4)]
+    pre, normals = [], []
+    for i, at in enumerate(cuts):
+        pre.append(x[at].astype(F32) + nn(ctx[at], ow_ref[...]) + line(ob_ref))
+        if i:
+            normals.append(norm(pre[i - 1]))
+    normals.append(norm(pre[-1]))
+    xh1 = jnp.concatenate([a for a, _ in normals], axis=0)
+    rs1 = jnp.concatenate([b for _, b in normals], axis=0)
     normed = xh1 * line(g1_ref) + line(s1_ref)
     low = normed.astype(BF)
     put(low_ref, low)
@@ -219,7 +228,13 @@
         for copy in weights:
             copy.wait()
 
-    for c in range(depth // width):
+    def up_of(c):
+        cols = slice(c * width, (c + 1) * width)
+        return nn(low, uw_ref[:, cols]) + ub_ref[cols].reshape(1, width)
+
+    chunks = depth // width
+    ahead = up_of(0)
+    for c in range(chunks):
         if c == 2:
 
             @pl.when(step == 0)
@@ -240,7 +255,9 @@
                 core_copy.start()
 
         cols = slice(c * width, (c + 1) * width)
-        up = nn(low, uw_ref[:, cols]) + ub_ref[cols].reshape(1, width)
+        up = ahead
+        if c + 1 < chunks:
+            ahead = up_of(c + 1)
         cdf = 0.5 * (lax.erf(up * 0.7071067811865476) + 1.0)
         slope = cdf + up * (0.3989422804014327 * jnp.exp(-0.5 * up * up))
         hidden = (up * cdf).astype(BF)

time: 222 us -> 219 us (0.986)
  Pallas kernels: 221 us -> 218 us
    pallas_call x1, Pallas kernels: 44.3 us -> 41.6 us  [forward(): pl.pallas_call(forward_kernel, grid=(4,), in_specs=[tile(width), tile(wid...]
where the time goes in v3:
time: 219 us
  Pallas kernels  218 us (100%)
    pallas_call x1, Pallas kernels, tail(): pl.pallas_call(functools.partial(tail_kernel, fused, nz), grid=(STEPS,),...  86.2 us
    pallas_call x1, Pallas kernels, backward(): pl.pallas_call(functools.partial(backward_kernel, fused, nz), grid=(8,),...  51.6 us
    pallas_call x1, Pallas kernels, forward(): pl.pallas_call(forward_kernel, grid=(4,), in_specs=[tile(width), tile(wid...  41.6 us
    pallas_call x1, Pallas kernels, attend(): pl.pallas_call(attend_kernel, grid=(sents // SIDE,), in_specs=[pl.BlockSp...  18.7 us
    pallas_call x1, Pallas kernels, ranking(): pl.pallas_call(ranking_kernel, grid=(sents // SIDE,), in_specs=[resident(...  12.8 us
    pallas_call x1, Pallas kernels, finish(): pl.pallas_call(functools.partial(finish_kernel, fused), grid=(TILES,), in...  7.01 us

profile of v3, /device:TPU:0, one launch (start us, length us, event | category | flops | bytes accessed | tf_op | source)
XLA Modules:
  0.0 218.8 jit_solution(14013197491659271064)
XLA Ops:
  0.6 18.7 %attend.1 = (bf16[2048,2304]{1,0:T(8,128)(2,1)}, bf16[32,64,768]{2,1,0:T(8,128)(2,1)}, bf16[2048,768]{1,0:T(8,128)(2,1)}) custom-call(bf16[32,64,768]{2,1,0:T(8,128)(2,1)} %x_ref.3, bf16[768,2304]{1,0:T(8,128)(2,1)} %refs_8_.3, f32[768]{0:T(1024)} %qb_ref.1, f32[768]{0:T(1024)} %vb_ref.1), custom_call_target="tpu_custom_call" | custom-call | tf_op jit(solution)/shard_map/attend/pallas_call | solution.py:112
  19.4 41.6 %forward.1 = (bf16[32,64,768]{2,1,0:T(8,128)(2,1)}, bf16[32,64,768]{2,1,0:T(8,128)(2,1)}, f32[32,64,128]{2,1,0:T(8,128)}, bf16[32,64,3072]{2,1,0:T(8,128)(2,1)},...) custom-call(bf16[32,64,768]{2,1,0:T(8,128)(2,1)} %x_ref.3, ...), custom_call_target="tpu_custom_call" | custom-call | tf_op jit(solution)/shard_map/forward/pallas_call | solution.py:309
  61.0 12.8 %ranking.1 = (f32[1,1]{1,0:T(1,128)}, bf16[32,64,768]{2,1,0:T(8,128)(2,1)}, bf16[2048,768]{1,0:T(8,128)(2,1)}, f32[8,768]{1,0:T(8,128)}) custom-call(bf16[2,512,768]{2,1,0:T(8,128)(2,1)} %bitcast.16, s32[512]{0:T(512)} %group_ref.1, f32[32,768]{1,0:T(8,128)} %get-tuple-element.61.cls_ref, bf16[32,64,768]{2,1,0:T(8,128)(2,1)} %cot_ref.1, ...), custom_call_target="tpu_custom_call" | custom-call | tf_op jit(solution)/shard_map/ranking/pallas_call | solution.py:429
  73.7 51.6 %backward.1 = (bf16[2048,3072]{1,0:T(8,128)(2,1)}, bf16[2048,768]{1,0:T(8,128)(2,1)}, bf16[2048,768]{1,0:T(8,128)(2,1)}, f32[8,768]{1,0:T(8,128)}, f32[1,3072]{1...) custom-call(bf16[2048,768]{1,0:T(8,128)(2,1)} %get-tuple-element.67.refs_0_, ...), custom_call_target="tpu_custom_call" | custom-call | tf_op jit(solution)/shard_map/backward/pallas_call | solution.py:713
  125.3 86.2 %tail.1 = (bf16[2048,768]{1,0:T(8,128)(2,1)}, f32[16,768]{1,0:T(8,128)}, bf16[8,48,384]{2,1,0:T(8,128)(2,1)}, bf16[8,48,384]{2,1,0:T(8,128)(2,1)}, bf16[192,384]{1,0:T(8,128)(2,1)}, /*index=5*/bf16[192,384]{1,0:T(8,128)(2,1)}) custom-call(bf16[2048,768]{1,0:T(8,128)(2,1)} %bitcast.14, bf16[2048,3072]{1,0:T(8,128)(2,1)} %get-tuple-element.72.refs_1_, ...), custom_call_target="tpu_custom_call" | custom-call | tf_op jit(solution)/shard_map/tail/pallas_call | solution.py:1014
  211.6 7.0 %finish.1 = (f32[2048,768]{1,0:T(8,128)}, f32[48,2304]{1,0:T(8,128)}, f32[48]{0:T(128)}, f32[48]{0:T(128)}, f32[48,768]{1,0:T(8,128)}, /*index=5*/f32[48]{0:T(12...) custom-call(bf16[2048,768]{1,0:T(8,128)(2,1)} %get-tuple-element.81., ...), custom_call_target="tpu_custom_call" | custom-call | tf_op jit(solution)/shard_map/finish/pallas_call | solution.py:1085

commit v4 on v3

--- a/solution.py
+++ b/solution.py
@@ -858,10 +858,10 @@
             p = [v.astype(F32) for v in low]
             dctx = [blocked(dctx_ref[s * seq : (s + 1) * seq, :], mask) for s in which]
             d_probs = [nt(v_ref[s * seq : (s + 1) * seq, :], c) for s, c in zip(which, dctx, strict=True)]
-            d_scores = [
-                (a * (b - jnp.sum(a * b, axis=0, keepdims=True))).astype(BF) for a, b in zip(p, d_probs, strict=True)
-            ]
-            d_value = [nn(a, b).astype(BF) for a, b in zip(low, dctx, strict=True)]
+            d_scores, d_value = [], []
+            for a, b, v, c in zip(p, d_probs, low, dctx, strict=True):
+                d_value.append(nn(v, c).astype(BF))
+                d_scores.append((a * (b - jnp.sum(a * b, axis=0, keepdims=True))).astype(BF))
             d_query = [(paired(a, b, seq) * scale).astype(BF) for a, b in zip(d_scores, k, strict=True)]
             d_key = [
                 (nn(a, blocked(q_ref[s * seq : (s + 1) * seq, :], mask)) * scale).astype(BF)
@@ -1040,7 +1040,7 @@
     if not fused:
         return
 
-    @pl.when(pl.program_id(0) == 0)
+    @pl.when(pl.program_id(0) == 1)
     def _():
         wide, narrow, z, _, _ = place()
         width = vec_ref.shape[1]

time: 219 us -> 219 us (level)
  no operation moved by 1% of the time
where the time goes in v4:
time: 219 us
  Pallas kernels  218 us (100%)
    pallas_call x1, Pallas kernels, tail(): pl.pallas_call(functools.partial(tail_kernel, fused, nz), grid=(STEPS,),...  86.2 us
    pallas_call x1, Pallas kernels, backward(): pl.pallas_call(functools.partial(backward_kernel, fused, nz), grid=(8,),...  51.6 us
    pallas_call x1, Pallas kernels, forward(): pl.pallas_call(forward_kernel, grid=(4,), in_specs=[tile(width), tile(wid...  41.6 us
    pallas_call x1, Pallas kernels, attend(): pl.pallas_call(attend_kernel, grid=(sents // SIDE,), in_specs=[pl.BlockSp...  18.7 us
    pallas_call x1, Pallas kernels, ranking(): pl.pallas_call(ranking_kernel, grid=(sents // SIDE,), in_specs=[resident(...  12.8 us
    pallas_call x1, Pallas kernels, finish(): pl.pallas_call(functools.partial(finish_kernel, fused), grid=(TILES,), in...  6.89 us

profile of v4, /device:TPU:0, one launch (start us, length us, event | category | flops | bytes accessed | tf_op | source)
XLA Modules:
  0.0 218.7 jit_solution(1992819380144680693)
XLA Ops:
  0.6 18.7 %attend.1 = (bf16[2048,2304]{1,0:T(8,128)(2,1)}, bf16[32,64,768]{2,1,0:T(8,128)(2,1)}, bf16[2048,768]{1,0:T(8,128)(2,1)}) custom-call(bf16[32,64,768]{2,1,0:T(8,128)(2,1)} %x_ref.3, bf16[768,2304]{1,0:T(8,128)(2,1)} %refs_8_.3, f32[768]{0:T(1024)} %qb_ref.1, f32[768]{0:T(1024)} %vb_ref.1), custom_call_target="tpu_custom_call" | custom-call | tf_op jit(solution)/shard_map/attend/pallas_call | solution.py:112
  19.4 41.6 %forward.1 = (bf16[32,64,768]{2,1,0:T(8,128)(2,1)}, bf16[32,64,768]{2,1,0:T(8,128)(2,1)}, f32[32,64,128]{2,1,0:T(8,128)}, bf16[32,64,3072]{2,1,0:T(8,128)(2,1)},...) custom-call(bf16[32,64,768]{2,1,0:T(8,128)(2,1)} %x_ref.3, ...), custom_call_target="tpu_custom_call" | custom-call | tf_op jit(solution)/shard_map/forward/pallas_call | solution.py:309
  61.0 12.8 %ranking.1 = (f32[1,1]{1,0:T(1,128)}, bf16[32,64,768]{2,1,0:T(8,128)(2,1)}, bf16[2048,768]{1,0:T(8,128)(2,1)}, f32[8,768]{1,0:T(8,128)}) custom-call(bf16[2,512,768]{2,1,0:T(8,128)(2,1)} %bitcast.16, s32[512]{0:T(512)} %group_ref.1, f32[32,768]{1,0:T(8,128)} %get-tuple-element.61.cls_ref, bf16[32,64,768]{2,1,0:T(8,128)(2,1)} %cot_ref.1, ...), custom_call_target="tpu_custom_call" | custom-call | tf_op jit(solution)/shard_map/ranking/pallas_call | solution.py:429
  73.7 51.6 %backward.1 = (bf16[2048,3072]{1,0:T(8,128)(2,1)}, bf16[2048,768]{1,0:T(8,128)(2,1)}, bf16[2048,768]{1,0:T(8,128)(2,1)}, f32[8,768]{1,0:T(8,128)}, f32[1,3072]{1...) custom-call(bf16[2048,768]{1,0:T(8,128)(2,1)} %get-tuple-element.67.refs_0_, ...), custom_call_target="tpu_custom_call" | custom-call | tf_op jit(solution)/shard_map/backward/pallas_call | solution.py:713
  125.3 86.2 %tail.1 = (bf16[2048,768]{1,0:T(8,128)(2,1)}, f32[16,768]{1,0:T(8,128)}, bf16[8,48,384]{2,1,0:T(8,128)(2,1)}, bf16[8,48,384]{2,1,0:T(8,128)(2,1)}, bf16[192,384]{1,0:T(8,128)(2,1)}, /*index=5*/bf16[192,384]{1,0:T(8,128)(2,1)}) custom-call(bf16[2048,768]{1,0:T(8,128)(2,1)} %bitcast.14, bf16[2048,3072]{1,0:T(8,128)(2,1)} %get-tuple-element.72.refs_1_, ...), custom_call_target="tpu_custom_call" | custom-call | tf_op jit(solution)/shard_map/tail/pallas_call | solution.py:1014
  211.6 6.9 %finish.1 = (f32[2048,768]{1,0:T(8,128)}, f32[48,2304]{1,0:T(8,128)}, f32[48]{0:T(128)}, f32[48]{0:T(128)}, f32[48,768]{1,0:T(8,128)}, /*index=5*/f32[48]{0:T(12...) custom-call(bf16[2048,768]{1,0:T(8,128)(2,1)} %get-tuple-element.81., ...), custom_call_target="tpu_custom_call" | custom-call | tf_op jit(solution)/shard_map/finish/pallas_call | solution.py:1085
